TPU v7x, 32 devices: a whole 2x2x4 slice. The times are simulated.
32 devices in a mesh: sub: 4 (over x, core), beam: 4 (over z), comp: 2 (over y).
Axes of the slice: x: 2, y: 2, z: 4, core: 2. Of those that a mesh axis runs over, the one named last changes fastest.
Arguments:
- raw_pulses: bfloat16 [4096, 2, 16384], P(('sub', 'beam', 'comp')), may hold values from -6 to 6
- range_filter: float32 [2, 16384], replicated, may hold values from -4 to 4
- steer_angle: float32 [64, 4096], P(None, ('sub', 'beam', 'comp')), may hold values from -3.140625 to 3.140625
- band_offsets: int32 [2, 384], P(None, ('beam', 'comp')), may hold values from -4 to 12, as said below
- band_weights: float32 [2, 384, 8], P(None, ('beam', 'comp')), may hold values from -1.5 to 1.5
- beam_delay: float32 [2, 384], P(None, ('beam', 'comp')), may hold values from -3 to 3
Outputs:
- scene_beams: float32 [256, 2, 16384], P(('beam', 'comp'), None, 'sub')
Inputs may be any that keep to these rules, and one draw needn't show every extreme that they name: `band_offsets`: for new beam u of a merge level l and a block (0 <= u < 2 * 8 2^l), each side's offset is u // 2 - 8 // 2 + 1 or one less; the first beam of every level and block takes the lesser value, the last the greater.
All inputs are finite; a program needn't handle non-finite values.
Results may differ from a plain program's by a relative error of at most 0.0059.
Values may be sent and summed in bfloat16 or wider, within the bound.
A program may use at most 128 MiB of HBM per device.

v0:
```python
import math

import jax
import jax.numpy as jnp
from jax import lax
from jax.sharding import PartitionSpec as P

NR = 16384
RADIX = 128
BAND = 8


def from_partner(block, axis, bit):
    count = lax.axis_size(axis)
    route = []
    for low in range(count):
        high = low | 1 << bit
        if high != low and high < count:
            route += [(low, high), (high, low)]
    return lax.ppermute(block, axis, route)


def with_halo(block, sides, width):
    for axis, dim in sides:
        count = lax.axis_size(axis)
        forward = [(i, i + 1) for i in range(count - 1)]
        backward = [(target, source) for source, target in forward]
        low = lax.ppermute(
            lax.slice_in_dim(block, block.shape[dim] - width, None, axis=dim), axis, forward
        )
        high = lax.ppermute(lax.slice_in_dim(block, 0, width, axis=dim), axis, backward)
        block = jnp.concatenate([low, block, high], axis=dim)
    return block


def dft_table(length):
    index_row = jnp.arange(length, dtype=jnp.int32)
    product = index_row[:, None] * index_row[None, :] % length
    phase_angle = product.astype(jnp.float32) * (2.0 * math.pi / length)
    return (jnp.cos(phase_angle).astype(jnp.bfloat16), (-jnp.sin(phase_angle)).astype(jnp.bfloat16))


def real_form(length):
    cos_part, sin_part = dft_table(length)
    upper_rows = jnp.concatenate([cos_part, sin_part], axis=1)
    lower_rows = jnp.concatenate([-sin_part, cos_part], axis=1)
    return jnp.concatenate([upper_rows, lower_rows], axis=0)


def twiddle():
    freq_index = jnp.arange(RADIX, dtype=jnp.int32)[:, None]
    time_index = jnp.arange(RADIX, dtype=jnp.int32)[None, :]
    phase_angle = (freq_index * time_index % NR).astype(jnp.float32) * (2.0 * math.pi / NR)
    return (jnp.cos(phase_angle), -jnp.sin(phase_angle))


def compress(raw, range_filter):
    number = raw.shape[0]
    samples = raw.reshape(number, 2 * RADIX, RADIX)
    section_one = jnp.einsum(
        "pan,ak->pkn", samples, real_form(RADIX), preferred_element_type=jnp.float32
    )
    cos_part, sin_part = twiddle()
    real_in = section_one[:, :RADIX]
    imag_in = section_one[:, RADIX:]
    turned = jnp.stack(
        [real_in * cos_part - imag_in * sin_part, real_in * sin_part + imag_in * cos_part], 1
    )
    turned = turned.astype(jnp.bfloat16)
    second = real_form(RADIX).reshape(2, RADIX, 2, RADIX)
    spectrum = jnp.einsum("prkn,rnsm->psmk", turned, second, preferred_element_type=jnp.float32)
    spectrum = spectrum.reshape(number, 2, NR)
    factor = NR ** (-0.5)
    real_out = (spectrum[:, 0] * range_filter[0] - spectrum[:, 1] * range_filter[1]) * factor
    imag_out = (spectrum[:, 0] * range_filter[1] + spectrum[:, 1] * range_filter[0]) * factor
    return jnp.stack([real_out, imag_out], 1).astype(jnp.bfloat16)


def steering(phase_angle, factor):
    real_part = (jnp.cos(phase_angle) * factor).astype(jnp.bfloat16)
    imag_part = (jnp.sin(phase_angle) * factor).astype(jnp.bfloat16)
    return jnp.stack(
        [jnp.stack([real_part, -imag_part], -1), jnp.stack([imag_part, real_part], -1)], 1
    )


def beam_term(weights, pulses):
    return jnp.einsum("kspq,pqr->ksr", weights, pulses, preferred_element_type=jnp.float32)


def band_matrix(offset, weight, span):
    tap_index = offset[:, None] + BAND // 2 + jnp.arange(BAND, dtype=jnp.int32)[None, :]
    matches = tap_index[:, :, None] == jnp.arange(span, dtype=jnp.int32)[None, None, :]
    return jnp.sum(
        jnp.where(matches, weight[:, :, None], jnp.zeros_like(weight)[:, :, None]), axis=1
    )


def contribute(window, offset, weight, delay_row, range_rows):
    span = window.shape[0]
    matrix = band_matrix(offset, weight, span)
    blended = jnp.dot(
        matrix,
        window.reshape(span, -1),
        precision=lax.Precision.HIGHEST,
        preferred_element_type=jnp.float32,
    )
    blended = blended.reshape(offset.shape[0], 2, range_rows.shape[0], range_rows.shape[1])
    phase_angle = delay_row[:, None, None] * (1.0 + range_rows / NR)[None]
    cosine = jnp.cos(phase_angle)
    sine_part = jnp.sin(phase_angle)
    return (
        cosine * blended[:, 0] - sine_part * blended[:, 1],
        sine_part * blended[:, 0] + cosine * blended[:, 1],
    )


def body(raw_pulses, range_filter, steer_angle, band_offsets, band_weights, beam_delay):
    compressed = compress(raw_pulses, range_filter)
    beam_devices = lax.axis_size("beam")
    comp_devices = lax.axis_size("comp")
    blocks = beam_devices * comp_devices
    pulses_sub = raw_pulses.shape[0] * blocks
    factor = float(pulses_sub) ** (-0.5)
    first_beams = steer_angle.shape[0] // blocks
    weights = steering(steer_angle, factor)
    sub_count = lax.axis_size("sub")
    levels = sub_count.bit_length() - 1
    sub_index = lax.axis_index("sub")
    subimage = lax.psum_scatter(
        beam_term(weights, compressed), ("beam", "comp"), scatter_dimension=0, tiled=True
    )
    margin = BAND // 2
    block_rows = NR // sub_count
    beam_count = first_beams
    subimage = subimage.reshape(beam_count, 2, sub_count, block_rows)
    for level_index in range(levels):
        kept_blocks = subimage.shape[2] // 2
        parity = sub_index >> level_index & 1
        low_bits = sub_index & (1 << level_index) - 1
        halves = subimage.reshape(beam_count, 2, kept_blocks, 2, block_rows)
        own_plain = lax.dynamic_index_in_dim(halves, parity, 3, keepdims=False)
        for_peer = lax.dynamic_index_in_dim(halves, 1 - parity, 3, keepdims=False)
        peer_plain = from_partner(for_peer, "sub", level_index)
        children = with_halo(
            jnp.stack([own_plain, peer_plain], 1), ((("beam", "comp"), 0),), margin
        )
        own_child = children[:, 0]
        peer_child = children[:, 1]
        new_beams = 2 * beam_count
        column_base = first_beams * (2 ** (level_index + 1) - 2)
        level_offsets = band_offsets[:, column_base : column_base + new_beams]
        level_weights = band_weights[:, column_base : column_base + new_beams]
        level_delays = beam_delay[:, column_base : column_base + new_beams]
        block_ids = jnp.arange(kept_blocks, dtype=jnp.int32)
        block_starts = (
            block_ids << level_index + 1 | parity << level_index | low_bits
        ) * block_rows
        range_rows = (
            block_starts[:, None] + jnp.arange(block_rows, dtype=jnp.int32)[None, :]
        ).astype(jnp.float32)
        real_own, imag_own = contribute(
            own_child,
            lax.dynamic_index_in_dim(level_offsets, parity, 0, keepdims=False),
            lax.dynamic_index_in_dim(level_weights, parity, 0, keepdims=False),
            lax.dynamic_index_in_dim(level_delays, parity, 0, keepdims=False),
            range_rows,
        )
        real_peer, imag_peer = contribute(
            peer_child,
            lax.dynamic_index_in_dim(level_offsets, 1 - parity, 0, keepdims=False),
            lax.dynamic_index_in_dim(level_weights, 1 - parity, 0, keepdims=False),
            lax.dynamic_index_in_dim(level_delays, 1 - parity, 0, keepdims=False),
            range_rows,
        )
        subimage = jnp.stack([real_own + real_peer, imag_own + imag_peer], 1)
        beam_count = new_beams
    return subimage.reshape(beam_count, 2, block_rows)


def solution(mesh):
    in_specs = (
        P(("sub", "beam", "comp"), None, None),
        P(),
        P(None, ("sub", "beam", "comp")),
        P(None, ("beam", "comp")),
        P(None, ("beam", "comp"), None),
        P(None, ("beam", "comp")),
    )
    out_specs = P(("beam", "comp"), None, "sub")
    return jax.shard_map(body, mesh=mesh, in_specs=in_specs, out_specs=out_specs, check_vma=False)
```

profile of v0, /device:TPU:8, one launch (start us, length us, event | category | flops | bytes accessed | tf_op | source)
XLA Modules:
  0.0 320.6 jit_solution(16581025476976545591)
XLA Ops:
  6.5 0.3 negate_convert_fusion
  6.8 0.3 fusion.68
  7.1 0.3 fusion.66
  7.4 0.3 sine_negate_fusion
  7.6 0.9 fusion.73
  8.5 0.9 negate_bitcast_fusion
  9.4 14.5 %reshape.528 = bf16[128,256,128]{2,1,0:T(8,128)(2,1)} reshape(bf16[128,2,16384]{2,1,0:T(2,128)(2,1)} %param.6) | data formatting | bytes 16777216 | tf_op jit(solution)/shard_map/reshape | solution.py:59
  24.0 11.5 %convolution_bitcast_fusion.1 = f32[128,256,128]{2,1,0:T(8,128)} fusion(bf16[128,256,128]{2,1,0:T(8,128)(2,1)} %reshape.528, bf16[128,128]{0,1:T(8,128)(2,1)S(1)} %get-tuple-element.44, bf16[128,128]{0,1:T(8,128)(2,1)S(1)} %fusion.68, bf16[128,128]{0,1:T(8,128)(2,1)S(1)} %get-tuple-element.43), kind=kOutput, calls=%fused_computation.1 | convolution fusion | flops 2148007936 | bytes 25264128 | tf_op jit(solution)/shard_map/pan,ak->pkn/dot_general | solution.py:60
  35.7 7.0 %fusion.8 = (bf16[128,1,128,128]{3,2,0,1:T(8,128)(2,1)S(1)}, bf16[128,1,128,128]{3,2,0,1:T(8,128)(2,1)S(1)}) fusion(f32[128,256,128]{2,1,0:T(8,128)} %convolution_bitcast_fusion.1, f32[128,128]{1,0:T(8,128)S(1)} %copy.33, f32[128,128]{1,0:T(8,128)S(1)} %copy.32), kind=kLoop, calls=%fused_computation.16 | loop fusion | flops 16777216 | bytes 25296896 | tf_op jit(solution)/shard_map/stack | solution.py:66
  42.7 7.0 %fusion.5 = f32[128,2,128,128]{3,2,0,1:T(8,128)} fusion(bf16[2,128,2,128,1]{1,0,3,2,4:T(2,128)(2,1)S(1)} %bitcast.155, bf16[128,1,128,128]{3,2,0,1:T(8,128)(2,1)S(1)} %get-tuple-element.8, bf16[128,1,128,128]{3,2,0,1:T(8,128)(2,1)S(1)} %get-tuple-element.7), kind=kOutput, calls=%fused_computation.13 | convolution fusion | flops 2151677952 | bytes 25296896 | tf_op jit(solution)/shard_map/prkn,rnsm->psmk/dot_general | solution.py:71
  49.7 18.3 %reshape.529 = f32[128,2,16384]{2,0,1:T(8,128)} reshape(f32[128,2,128,128]{3,2,0,1:T(8,128)} %fusion.5) | data formatting | bytes 33554432 | tf_op jit(solution)/shard_map/reshape | solution.py:72
  68.1 7.1 %multiply_convert_fusion.1 = (bf16[128,1,16384]{2,0,1:T(8,128)(2,1)S(1)}, bf16[128,1,16384]{2,0,1:T(8,128)(2,1)S(1)}) fusion(f32[128,2,16384]{2,0,1:T(8,128)} %reshape.529, f32[16384]{0:T(1024)S(1)} %bitcast.154, f32[16384]{0:T(1024)S(1)} %bitcast.153), kind=kLoop, calls=%fused_computation.10 | loop fusion | flops 20971520 | bytes 25296896 | tf_op jit(solution)/shard_map/convert
  75.3 4.0 %convolution_bitcast_fusion = f32[64,2,16384]{2,0,1:T(8,128)} fusion(bf16[128,1,16384]{2,0,1:T(8,128)(2,1)S(1)} %get-tuple-element.6, bf16[128,1,16384]{2,0,1:T(8,128)(2,1)S(1)} %get-tuple-element.5, bf16[64,1,128,2]{2,0,3,1:T(8,128)(2,1)S(1)} %get-tuple-element.30, bf16[64,1,128,2]{2,0,3,1:T(8,128)(2,1)S(1)} %get-tuple-element.29), kind=kOutput, calls=%fused_computation | convolution fusion | flops 1077968896 | bytes 16842752 | tf_op jit(solution)/shard_map/kspq,pqr->ksr/dot_general | solution.py:88
  79.3 0.7 copy-done.1
  80.4 146.7 %reduce-scatter.2.cloned.1.call-done = f32[8,2,16384]{2,0,1:T(8,128)} async-done(((f32[64,2,16384]{2,0,1:T(8,128)}), f32[8,2,16384]{2,0,1:T(8,128)}) %reduce-scatter.2.cloned.1.call-update) | async-done | bytes 1048592 | tf_op jit(solution)/shard_map/reduce_scatter | solution.py:130
  227.1 1.3 constant_dynamic-slice_fusion.7
  228.3 0.4 copy.85
  228.9 0.1 select_reduce_fusion.3
  229.0 0.1 select_reduce_fusion.2
  229.2 0.4 copy.86
  229.6 1.2 collective-permute-done
  230.7 0.5 fusion.46
  231.3 3.4 %collective-permute-start.1 = (f32[4,2,2,2,4096]{4,3,2,0,1:T(2,128)S(1)}, f32[4,2,2,2,4096]{4,3,2,0,1:T(2,128)S(1)}, u32[]{:S(2)}, u32[]{:S(2)}) collective-permute-start(f32[4,2,2,2,4096]{4,3,2,0,1:T(2,128)S(1)} %get-tuple-element.21), channel_id=1, source_target_pairs={{0,1},{1,2},{2,3},{3,4},{4,5},{5,6},{6,7},{8,9},{9,10},{10,11},{11... | collective-permute-start | bytes 1572872 | tf_op jit(solution)/shard_map/ppermute | solution.py:28
  234.7 3.5 %collective-permute-start.2 = (f32[4,2,2,2,4096]{4,3,2,0,1:T(2,128)S(1)}, f32[4,2,2,2,4096]{4,3,2,0,1:T(2,128)S(1)}, u32[]{:S(2)}, u32[]{:S(2)}) collective-permute-start(f32[4,2,2,2,4096]{4,3,2,0,1:T(2,128)S(1)} %get-tuple-element.22), channel_id=1, source_target_pairs={{1,0},{2,1},{3,2},{4,3},{5,4},{6,5},{7,6},{9,8},{10,9},{11,10},{12... | collective-permute-start | bytes 1572872 | tf_op jit(solution)/shard_map/ppermute | solution.py:31
  238.3 19.0 %collective-permute-done.1 = f32[4,2,2,2,4096]{4,3,2,0,1:T(2,128)S(1)} collective-permute-done((f32[4,2,2,2,4096]{4,3,2,0,1:T(2,128)S(1)}, f32[4,2,2,2,4096]{4,3,2,0,1:T(2,128)S(1)}, u32[]{:S(2)}, u32[]{:S(2)}) %collective-permute-start.1) | collective-permute-done | bytes 524320 | tf_op jit(solution)/shard_map/ppermute | solution.py:28
  257.4 1.9 collective-permute-done.2
  259.3 1.3 pad_maximum_fusion.1
  260.6 1.1 fusion.91
  261.7 0.9 reshape_squeeze.12
  262.6 0.9 dot_general.41
  263.5 2.1 reshape_squeeze.13
  265.6 0.9 dot_general.44
  266.5 1.5 fusion.12
  268.0 1.5 fusion.10
  269.5 4.0 %fusion.41 = (f32[16,1,2,4096]{3,0,2,1:T(8,128)S(1)}, f32[16,1,2,4096]{3,0,2,1:T(8,128)S(1)}) fusion(f32[16,2,2,4096]{3,0,2,1:T(8,128)S(1)} %fusion.10, f32[16,2,2,4096]{3,0,2,1:T(8,128)S(1)} %fusion.12, f32[16]{0:T(128)S(1)} %get-tuple-element.40, f32[2,4096]{1,0:T(2,128)S(1)} %multiply_add_fusion, f32[16]{0:T(128)S(1)} %get-tuple-element.39), kind=kLoop, calls=%fused_computation.66 | loop fusion | flops 2097152 | bytes 3178624 | tf_op jit(solution)/shard_map/add | solution.py:176
  273.6 1.5 collective-permute-start.3
  275.2 12.4 %collective-permute-done.3 = f32[16,2,1,4096]{3,0,2,1:T(8,128)S(1)} collective-permute-done((f32[16,2,1,4096]{3,0,2,1:T(8,128)S(1)}, f32[16,2,1,4096]{3,0,2,1:T(8,128)S(1)}, u32[]{:S(2)}, u32[]{:S(2)}) %collective-permute-start.3) | collective-permute-done | bytes 524320 | tf_op jit(solution)/shard_map/ppermute | solution.py:20
  287.6 1.9 collective-permute-start.4
  289.6 5.0 %collective-permute-start.5 = (f32[4,2,2,1,4096]{4,0,2,3,1:T(4,128)S(1)}, f32[4,2,2,1,4096]{4,0,2,3,1:T(4,128)S(1)}, u32[]{:S(2)}, u32[]{:S(2)}) collective-permute-start(f32[4,2,2,1,4096]{4,0,2,3,1:T(4,128)S(1)} %get-tuple-element.18), channel_id=1, source_target_pairs={{1,0},{2,1},{3,2},{4,3},{5,4},{6,5},{7,6},{9,8},{10,9},{11,10},{12... | collective-permute-start | bytes 786440 | tf_op jit(solution)/shard_map/ppermute | solution.py:31
  294.7 5.7 %collective-permute-done.4 = f32[4,2,2,1,4096]{4,0,2,3,1:T(4,128)S(1)} collective-permute-done((f32[4,2,2,1,4096]{4,0,2,3,1:T(4,128)S(1)}, f32[4,2,2,1,4096]{4,0,2,3,1:T(4,128)S(1)}, u32[]{:S(2)}, u32[]{:S(2)}) %collective-permute-start.4) | collective-permute-done | bytes 262176 | tf_op jit(solution)/shard_map/ppermute | solution.py:28
  300.4 3.1 collective-permute-done.5
  303.4 0.2 pad_maximum_fusion.2
  303.8 0.6 copy.41
  304.4 0.6 copy.43
  305.0 1.4 convolution_bitcast_fusion.3
  306.4 1.4 convolution_bitcast_fusion.2
  307.9 4.1 %fusion.35 = (f32[32,1,1,4096]{3,0,1,2:T(8,128)S(1)}, f32[32,1,1,4096]{3,0,1,2:T(8,128)S(1)}) fusion(f32[32,2,1,4096]{3,0,1,2:T(8,128)S(1)} %convolution_bitcast_fusion.2, f32[32,2,1,4096]{3,0,1,2:T(8,128)S(1)} %convolution_bitcast_fusion.3, f32[32]{0:T(128)S(1)} %get-tuple-element.36, f32[4096]{0:T(1024)S(1)} %multiply_add_fusion.1, f32[32]{0:T(128)S(1)} %get-tuple-element.35), kind=kLoop, calls=%fused_computation.60 | loop fusion | flops 2097152 | bytes 3162368 | tf_op jit(solution)/shard_map/add | solution.py:176
  312.0 1.8 copy.45
  (38 shorter events, 1.4 us)
Async XLA Ops:
  6.5 220.5 %reduce-scatter.2.cloned.1.call-start = ((), (), s32[]{:S(2)}) async-start(), calls=%async_computation.1 | async-start | bytes 9437184 | tf_op jit(solution)/shard_map/reduce_scatter | solution.py:130
  49.7 18.3 %copy-start = (f32[2,16384]{1,0:T(2,128)S(1)}, f32[2,16384]{1,0:T(2,128)}, u32[]{:S(2)}) copy-start(f32[2,16384]{1,0:T(2,128)} %param.7) | copy-start | bytes 393220
  79.3 0.7 copy-start.1
  79.3 0.9 copy-start.2
  79.3 1.0 copy-start.3
  228.8 2.0 collective-permute-start
  231.3 26.1 %collective-permute-start.1 = (f32[4,2,2,2,4096]{4,3,2,0,1:T(2,128)S(1)}, f32[4,2,2,2,4096]{4,3,2,0,1:T(2,128)S(1)}, u32[]{:S(2)}, u32[]{:S(2)}) collective-permute-start(f32[4,2,2,2,4096]{4,3,2,0,1:T(2,128)S(1)} %get-tuple-element.21), channel_id=1, source_target_pairs={{0,1},{1,2},{2,3},{3,4},{4,5},{5,6},{6,7},{8,9},{9,10},{10,11},{11... | collective-permute-start | bytes 1572872 | tf_op jit(solution)/shard_map/ppermute | solution.py:28
  234.7 24.6 %collective-permute-start.2 = (f32[4,2,2,2,4096]{4,3,2,0,1:T(2,128)S(1)}, f32[4,2,2,2,4096]{4,3,2,0,1:T(2,128)S(1)}, u32[]{:S(2)}, u32[]{:S(2)}) collective-permute-start(f32[4,2,2,2,4096]{4,3,2,0,1:T(2,128)S(1)} %get-tuple-element.22), channel_id=1, source_target_pairs={{1,0},{2,1},{3,2},{4,3},{5,4},{6,5},{7,6},{9,8},{10,9},{11,10},{12... | collective-permute-start | bytes 1572872 | tf_op jit(solution)/shard_map/ppermute | solution.py:31
  273.6 13.9 %collective-permute-start.3 = (f32[16,2,1,4096]{3,0,2,1:T(8,128)S(1)}, f32[16,2,1,4096]{3,0,2,1:T(8,128)S(1)}, u32[]{:S(2)}, u32[]{:S(2)}) collective-permute-start(f32[16,2,1,4096]{3,0,2,1:T(8,128)S(1)} %get-tuple-element.20), channel_id=1, source_target_pairs={{0,16},{16,0},{8,24},{24,8},{1,17},{17,1},{9,25},{25,9},{2,18},{18... | collective-permute-start | bytes 1572872 | tf_op jit(solution)/shard_map/ppermute | solution.py:20
  287.6 12.7 %collective-permute-start.4 = (f32[4,2,2,1,4096]{4,0,2,3,1:T(4,128)S(1)}, f32[4,2,2,1,4096]{4,0,2,3,1:T(4,128)S(1)}, u32[]{:S(2)}, u32[]{:S(2)}) collective-permute-start(f32[4,2,2,1,4096]{4,0,2,3,1:T(4,128)S(1)} %get-tuple-element.17), channel_id=1, source_target_pairs={{0,1},{1,2},{2,3},{3,4},{4,5},{5,6},{6,7},{8,9},{9,10},{10,11},{11... | collective-permute-start | bytes 786440 | tf_op jit(solution)/shard_map/ppermute | solution.py:28
  289.6 13.9 %collective-permute-start.5 = (f32[4,2,2,1,4096]{4,0,2,3,1:T(4,128)S(1)}, f32[4,2,2,1,4096]{4,0,2,3,1:T(4,128)S(1)}, u32[]{:S(2)}, u32[]{:S(2)}) collective-permute-start(f32[4,2,2,1,4096]{4,0,2,3,1:T(4,128)S(1)} %get-tuple-element.18), channel_id=1, source_target_pairs={{1,0},{2,1},{3,2},{4,3},{5,4},{6,5},{7,6},{9,8},{10,9},{11,10},{12... | collective-permute-start | bytes 786440 | tf_op jit(solution)/shard_map/ppermute | solution.py:31
Sparse Core Ops, SparseCore 0:
  79.4 147.5 reduce-scatter.1
where the time goes:
time: 322 us; the launch traced here: 321 us
  waiting for transfers between devices  190 us (59%)
  local copies, waits for them, and re-layouts  45.3 us (14%)
  matrix products  28.3 us (9%)
  other arithmetic  27.9 us (9%)
  starting transfers between devices  15.5 us (5%)
  between operations  13.8 us (4%)
    reduce_scatter x1, waiting for transfers between devices, body(): lax.psum_scatter(beam_term(weights, compressed), ('beam', 'comp'), scatte...  147 us
    ppermute x2, waiting for transfers between devices, with_halo(): lax.ppermute(lax.slice_in_dim(block, block.shape[dim] - width, None, axis...  24.7 us
    reshape x1, local copies, waits for them, and re-layouts, compress(): spectrum = spectrum.reshape(number, 2, NR)  18.3 us
    reshape x1, local copies, waits for them, and re-layouts, compress(): samples = raw.reshape(number, 2 * RADIX, RADIX)  14.5 us
    ppermute x2, waiting for transfers between devices, from_partner(): return lax.ppermute(block, axis, route)  13.5 us
    dot_general x1, matrix products, compress(): jnp.einsum('pan,ak->pkn', samples, real_form(RADIX), preferred_element_ty...  11.5 us
    ppermute x2, starting transfers between devices, with_halo(): lax.ppermute(lax.slice_in_dim(block, 0, width, axis=dim), axis, backward)  8.59 us
    add x2, other arithmetic, body(): subimage = jnp.stack([real_own + real_peer, imag_own + imag_peer], 1)  8.1 us
  transfers between devices with their start and end apart: 7, of which 7 were waited for; matrix products, arithmetic and copies ran while one was open for 0% of the time, Pallas kernels for 0%

commit v1 on v0

--- a/solution.py
+++ b/solution.py
@@ -54,9 +54,9 @@
     return (jnp.cos(phase_angle), -jnp.sin(phase_angle))
 
 
-def compress(raw, range_filter):
-    number = raw.shape[0]
-    samples = raw.reshape(number, 2 * RADIX, RADIX)
+def compress(beams, range_filter):
+    number = beams.shape[0]
+    samples = beams.reshape(number, 2 * RADIX, RADIX)
     section_one = jnp.einsum(
         "pan,ak->pkn", samples, real_form(RADIX), preferred_element_type=jnp.float32
     )
@@ -66,14 +66,16 @@
     turned = jnp.stack(
         [real_in * cos_part - imag_in * sin_part, real_in * sin_part + imag_in * cos_part], 1
     )
-    turned = turned.astype(jnp.bfloat16)
     second = real_form(RADIX).reshape(2, RADIX, 2, RADIX)
-    spectrum = jnp.einsum("prkn,rnsm->psmk", turned, second, preferred_element_type=jnp.float32)
+    high = turned.astype(jnp.bfloat16)
+    low = (turned - high.astype(jnp.float32)).astype(jnp.bfloat16)
+    spectrum = jnp.einsum("prkn,rnsm->psmk", high, second, preferred_element_type=jnp.float32)
+    spectrum += jnp.einsum("prkn,rnsm->psmk", low, second, preferred_element_type=jnp.float32)
     spectrum = spectrum.reshape(number, 2, NR)
     factor = NR ** (-0.5)
     real_out = (spectrum[:, 0] * range_filter[0] - spectrum[:, 1] * range_filter[1]) * factor
     imag_out = (spectrum[:, 0] * range_filter[1] + spectrum[:, 1] * range_filter[0]) * factor
-    return jnp.stack([real_out, imag_out], 1).astype(jnp.bfloat16)
+    return jnp.stack([real_out, imag_out], 1)
 
 
 def steering(phase_angle, factor):
@@ -101,7 +103,7 @@
     matrix = band_matrix(offset, weight, span)
     blended = jnp.dot(
         matrix,
-        window.reshape(span, -1),
+        window.reshape(span, -1).astype(jnp.float32),
         precision=lax.Precision.HIGHEST,
         preferred_element_type=jnp.float32,
     )
@@ -116,7 +118,6 @@
 
 
 def body(raw_pulses, range_filter, steer_angle, band_offsets, band_weights, beam_delay):
-    compressed = compress(raw_pulses, range_filter)
     beam_devices = lax.axis_size("beam")
     comp_devices = lax.axis_size("comp")
     blocks = beam_devices * comp_devices
@@ -127,9 +128,9 @@
     sub_count = lax.axis_size("sub")
     levels = sub_count.bit_length() - 1
     sub_index = lax.axis_index("sub")
-    subimage = lax.psum_scatter(
-        beam_term(weights, compressed), ("beam", "comp"), scatter_dimension=0, tiled=True
-    )
+    partial = beam_term(weights, raw_pulses).astype(jnp.bfloat16)
+    summed = lax.psum_scatter(partial, ("beam", "comp"), scatter_dimension=0, tiled=True)
+    subimage = compress(summed, range_filter)
     margin = BAND // 2
     block_rows = NR // sub_count
     beam_count = first_beams
@@ -138,7 +139,7 @@
         kept_blocks = subimage.shape[2] // 2
         parity = sub_index >> level_index & 1
         low_bits = sub_index & (1 << level_index) - 1
-        halves = subimage.reshape(beam_count, 2, kept_blocks, 2, block_rows)
+        halves = subimage.astype(jnp.bfloat16).reshape(beam_count, 2, kept_blocks, 2, block_rows)
         own_plain = lax.dynamic_index_in_dim(halves, parity, 3, keepdims=False)
         for_peer = lax.dynamic_index_in_dim(halves, 1 - parity, 3, keepdims=False)
         peer_plain = from_partner(for_peer, "sub", level_index)

time: 322 us -> 184 us (0.57)
  waiting for transfers between devices: 190 us -> 109 us
  local copies, waits for them, and re-layouts: 45.3 us -> 11.7 us
  other arithmetic: 27.9 us -> 14.8 us
  matrix products: 28.3 us -> 18.1 us
    reduce_scatter x1 -> x0, waiting for transfers between devices: 147 us -> none  [body(): lax.psum_scatter(beam_term(weights, compressed), ('beam', 'comp'), scatte...]
    unnamed x1 -> x2, waiting for transfers between devices: 0.02 us -> 88.1 us
    reshape x1, local copies, waits for them, and re-layouts: 18.3 us -> 0.19 us  [compress(): spectrum = spectrum.reshape(number, 2, NR)]
    ppermute x2, waiting for transfers between devices: 24.7 us -> 8.74 us  [with_halo(): lax.ppermute(lax.slice_in_dim(block, block.shape[dim] - width, None, axis...]
    reshape x1, local copies, waits for them, and re-layouts: 14.5 us -> 0.39 us  [compress(): samples = beams.reshape(number, 2 * RADIX, RADIX)]
    dot_general x1, matrix products: 11.5 us -> 0.3 us  [compress(): jnp.einsum('pan,ak->pkn', samples, real_form(RADIX), preferred_element_ty...]
    dot_general x1, matrix products: 4.02 us -> 13.1 us  [beam_term(): jnp.einsum('kspq,pqr->ksr', weights, pulses, preferred_element_type=jnp.f...]
    dot_general x5 -> x6, matrix products: 12.8 us -> 4.67 us  [the longest x4 4 us: contribute(): jnp.dot(matrix, window.reshape(span, -1).astype(jnp.float32), precision=l...]
  transfers between devices with their start and end apart: 7 -> 7, of which waited for: 7 -> 7; matrix products, arithmetic and copies ran while one was open for 0% -> 1% of each run, Pallas kernels for 0% -> 0%
where the time goes in v1:
time: 184 us; the launch traced here: 183 us
  waiting for transfers between devices  109 us (59%)
  matrix products  18.1 us (10%)
  starting transfers between devices  15.3 us (8%)
  other arithmetic  14.8 us (8%)
  between operations  13.8 us (8%)
  local copies, waits for them, and re-layouts  11.7 us (6%)
    unnamed x2, waiting for transfers between devices  88.1 us
    dot_general x1, matrix products, beam_term(): jnp.einsum('kspq,pqr->ksr', weights, pulses, preferred_element_type=jnp.f...  13.1 us
    ppermute x2, waiting for transfers between devices, with_halo(): lax.ppermute(lax.slice_in_dim(block, block.shape[dim] - width, None, axis...  8.74 us
    ppermute x2, starting transfers between devices, with_halo(): lax.ppermute(lax.slice_in_dim(block, 0, width, axis=dim), axis, backward)  8.38 us
    ppermute x2, waiting for transfers between devices, from_partner(): return lax.ppermute(block, axis, route)  7.73 us
    ppermute x2, starting transfers between devices, with_halo(): lax.ppermute(lax.slice_in_dim(block, block.shape[dim] - width, None, axis...  5.33 us
    another operation x2, other arithmetic  4.37 us
    ppermute x2, waiting for transfers between devices, with_halo(): lax.ppermute(lax.slice_in_dim(block, 0, width, axis=dim), axis, backward)  4.29 us
  transfers between devices with their start and end apart: 7, of which 7 were waited for; matrix products, arithmetic and copies ran while one was open for 1% of the time, Pallas kernels for 0%

profile of v1, /device:TPU:8, one launch (start us, length us, event | category | flops | bytes accessed | tf_op | source)
XLA Modules:
  0.0 182.6 jit_solution(10950378713893660111)
XLA Ops:
  6.5 0.9 fusion.77
  7.4 0.9 negate_bitcast_fusion
  8.3 13.1 %fusion.1 = bf16[2,8,8,16384]{3,2,1,0:T(8,128)(2,1)S(1)} fusion(bf16[128,2,16384]{2,1,0:T(2,128)(2,1)} %param.6, bf16[64,1,128,2]{2,0,3,1:T(8,128)(2,1)S(1)} %get-tuple-element.30, bf16[64,1,128,2]{2,0,3,1:T(8,128)(2,1)S(1)} %get-tuple-element.29), kind=kOutput, calls=%fused_computation.2 | convolution fusion | flops 1075871744 | bytes 12648448 | tf_op jit(solution)/shard_map/kspq,pqr->ksr/dot_general | solution.py:90
  21.4 2.3 %copy.93 = bf16[2,8,8,16384]{3,2,0,1:T(8,128)(2,1)} copy(bf16[2,8,8,16384]{3,2,1,0:T(8,128)(2,1)S(1)} %fusion.1) | data formatting | bytes 8388608
  23.8 0.3 fusion.70
  24.2 0.3 sine_negate_fusion
  24.5 0.3 fusion.72
  24.8 0.3 negate_convert_fusion
  25.5 88.1 %reduce-scatter.4.cloned.1.call-done = bf16[8,32768]{1,0:T(8,128)(2,1)} async-done(((bf16[64,32768]{1,0:T(8,128)(2,1)}), bf16[8,32768]{1,0:T(8,128)(2,1)}) %reduce-scatter.4.cloned.1.call-update) | async-done | bytes 524304
  113.6 1.8 copy.61
  115.4 0.4 reshape.538
  115.8 0.3 convolution_bitcast_fusion.5
  116.1 0.1 subtract_bitcast_fusion
  116.2 0.3 convolution_bitcast_fusion.3
  116.6 0.3 fusion.5
  116.9 0.2 reshape.539
  117.1 0.2 multiply_convert_fusion
  117.3 0.3 copy_dynamic-update-slice_fusion.1
  117.6 0.3 copy_dynamic-update-slice_fusion
  117.9 0.6 dynamic-slice_bitcast_fusion.1
  119.0 1.0 collective-permute-done
  120.1 0.8 fusion.49
  120.8 3.4 %collective-permute-start.1 = (bf16[4,2,2,2,4096]{4,3,2,0,1:T(2,128)(2,1)S(1)}, bf16[4,2,2,2,4096]{4,3,2,0,1:T(2,128)(2,1)S(1)}, u32[]{:S(2)}, u32[]{:S(2)}) collective-permute-start(bf16[4,2,2,2,4096]{4,3,2,0,1:T(2,128)(2,1)S(1)} %get-tuple-element.21), channel_id=1, source_target_pairs={{0,1},{1,2},{2,3},{3,4},{4,5},{5,6},{6,7},{8,9},{9,10},{10,11},{11... | collective-permute-start | bytes 786440 | tf_op jit(solution)/shard_map/ppermute | solution.py:28
  124.2 3.3 %collective-permute-start.2 = (bf16[4,2,2,2,4096]{4,3,2,0,1:T(2,128)(2,1)S(1)}, bf16[4,2,2,2,4096]{4,3,2,0,1:T(2,128)(2,1)S(1)}, u32[]{:S(2)}, u32[]{:S(2)}) collective-permute-start(bf16[4,2,2,2,4096]{4,3,2,0,1:T(2,128)(2,1)S(1)} %get-tuple-element.22), channel_id=1, source_target_pairs={{1,0},{2,1},{3,2},{4,3},{5,4},{6,5},{7,6},{9,8},{10,9},{11,10},{12... | collective-permute-start | bytes 786440 | tf_op jit(solution)/shard_map/ppermute | solution.py:31
  127.7 8.0 %collective-permute-done.1 = bf16[4,2,2,2,4096]{4,3,2,0,1:T(2,128)(2,1)S(1)} collective-permute-done((bf16[4,2,2,2,4096]{4,3,2,0,1:T(2,128)(2,1)S(1)}, bf16[4,2,2,2,4096]{4,3,2,0,1:T(2,128)(2,1)S(1)}, u32[]{:S(2)}, u32[]{:S(2)}) %collective-permute-start.1) | collective-permute-done | bytes 262176 | tf_op jit(solution)/shard_map/ppermute | solution.py:28
  135.7 1.9 %collective-permute-done.2 = bf16[4,2,2,2,4096]{4,3,2,0,1:T(2,128)(2,1)S(1)} collective-permute-done((bf16[4,2,2,2,4096]{4,3,2,0,1:T(2,128)(2,1)S(1)}, bf16[4,2,2,2,4096]{4,3,2,0,1:T(2,128)(2,1)S(1)}, u32[]{:S(2)}, u32[]{:S(2)}) %collective-permute-start.2) | collective-permute-done | bytes 262176 | tf_op jit(solution)/shard_map/ppermute | solution.py:31
  137.6 1.6 pad_maximum_fusion.1
  139.2 0.9 fusion.95
  140.2 0.4 reshape_squeeze.12
  140.6 0.4 dot_general.45
  140.9 0.4 reshape_squeeze.13
  141.4 0.4 dot_general.48
  141.7 1.0 fusion.41
  142.7 1.0 fusion.39
  143.7 4.2 %fusion.32 = (bf16[16,1,2,4096]{3,0,2,1:T(8,128)(2,1)S(1)}, bf16[16,1,2,4096]{3,0,2,1:T(8,128)(2,1)S(1)}) fusion(f32[16,2,2,4096]{3,0,2,1:T(8,128)S(1)} %fusion.39, f32[16,2,2,4096]{3,0,2,1:T(8,128)S(1)} %fusion.41, f32[16]{0:T(128)S(1)} %get-tuple-element.40, f32[2,4096]{1,0:T(2,128)S(1)} %multiply_add_fusion, f32[16]{0:T(128)S(1)} %get-tuple-element.39), kind=kLoop, calls=%fused_computation.55 | loop fusion | flops 2359296 | bytes 2654336 | tf_op jit(solution)/shard_map/convert.1
  148.0 1.5 collective-permute-start.3
  149.6 6.7 %collective-permute-done.3 = bf16[16,2,1,4096]{3,0,2,1:T(8,128)(2,1)S(1)} collective-permute-done((bf16[16,2,1,4096]{3,0,2,1:T(8,128)(2,1)S(1)}, bf16[16,2,1,4096]{3,0,2,1:T(8,128)(2,1)S(1)}, u32[]{:S(2)}, u32[]{:S(2)}) %collective-permute-start.3) | collective-permute-done | bytes 262176 | tf_op jit(solution)/shard_map/ppermute | solution.py:20
  156.4 1.9 %collective-permute-start.4 = (bf16[4,2,2,1,4096]{4,0,2,3,1:T(4,128)(2,1)S(1)}, bf16[4,2,2,1,4096]{4,0,2,3,1:T(4,128)(2,1)S(1)}, u32[]{:S(2)}, u32[]{:S(2)}) collective-permute-start(bf16[4,2,2,1,4096]{4,0,2,3,1:T(4,128)(2,1)S(1)} %get-tuple-element.17), channel_id=1, source_target_pairs={{0,1},{1,2},{2,3},{3,4},{4,5},{5,6},{6,7},{8,9},{9,10},{10,11},{11... | collective-permute-start | bytes 393224 | tf_op jit(solution)/shard_map/ppermute | solution.py:28
  158.3 5.0 %collective-permute-start.5 = (bf16[4,2,2,1,4096]{4,0,2,3,1:T(4,128)(2,1)S(1)}, bf16[4,2,2,1,4096]{4,0,2,3,1:T(4,128)(2,1)S(1)}, u32[]{:S(2)}, u32[]{:S(2)}) collective-permute-start(bf16[4,2,2,1,4096]{4,0,2,3,1:T(4,128)(2,1)S(1)} %get-tuple-element.18), channel_id=1, source_target_pairs={{1,0},{2,1},{3,2},{4,3},{5,4},{6,5},{7,6},{9,8},{10,9},{11,10},{12... | collective-permute-start | bytes 393224 | tf_op jit(solution)/shard_map/ppermute | solution.py:31
  163.4 0.7 collective-permute-done.4
  164.2 2.4 %collective-permute-done.5 = bf16[4,2,2,1,4096]{4,0,2,3,1:T(4,128)(2,1)S(1)} collective-permute-done((bf16[4,2,2,1,4096]{4,0,2,3,1:T(4,128)(2,1)S(1)}, bf16[4,2,2,1,4096]{4,0,2,3,1:T(4,128)(2,1)S(1)}, u32[]{:S(2)}, u32[]{:S(2)}) %collective-permute-start.5) | collective-permute-done | bytes 131104 | tf_op jit(solution)/shard_map/ppermute | solution.py:31
  166.6 0.3 pad_maximum_fusion.2
  166.9 0.4 copy.73
  167.4 0.4 copy.75
  167.8 1.0 convolution_bitcast_fusion.2
  168.8 1.0 convolution_bitcast_fusion.1
  169.8 4.1 %fusion.24 = (f32[32,1,1,4096]{3,0,1,2:T(8,128)S(1)}, f32[32,1,1,4096]{3,0,1,2:T(8,128)S(1)}) fusion(f32[32,2,1,4096]{3,0,1,2:T(8,128)S(1)} %convolution_bitcast_fusion.1, f32[32,2,1,4096]{3,0,1,2:T(8,128)S(1)} %convolution_bitcast_fusion.2, f32[32]{0:T(128)S(1)} %get-tuple-element.36, f32[4096]{0:T(1024)S(1)} %multiply_add_fusion.1, f32[32]{0:T(128)S(1)} %get-tuple-element.35), kind=kLoop, calls=%fused_computation.47 | loop fusion | flops 2097152 | bytes 3162368 | tf_op jit(solution)/shard_map/add | solution.py:177
  174.0 1.8 copy.77
  (41 shorter events, 1.6 us)
Async XLA Ops:
  6.5 107.1 %reduce-scatter.4.cloned.1.call-start = ((), (), s32[]{:S(2)}) async-start(), calls=%async_computation.1 | async-start | bytes 4718592
  23.8 1.4 copy-start.2
  23.8 1.4 copy-start.1
  23.8 1.6 copy-start
  116.6 2.0 %copy-start.3 = (f32[2,48]{1,0:T(2,128)S(1)}, f32[2,48]{1,0:T(2,128)}, u32[]{:S(2)}) copy-start(f32[2,48]{1,0:T(2,128)} %param.11) | copy-start | bytes 1156
  118.5 1.6 collective-permute-start
  120.8 14.9 %collective-permute-start.1 = (bf16[4,2,2,2,4096]{4,3,2,0,1:T(2,128)(2,1)S(1)}, bf16[4,2,2,2,4096]{4,3,2,0,1:T(2,128)(2,1)S(1)}, u32[]{:S(2)}, u32[]{:S(2)}) collective-permute-start(bf16[4,2,2,2,4096]{4,3,2,0,1:T(2,128)(2,1)S(1)} %get-tuple-element.21), channel_id=1, source_target_pairs={{0,1},{1,2},{2,3},{3,4},{4,5},{5,6},{6,7},{8,9},{9,10},{10,11},{11... | collective-permute-start | bytes 786440 | tf_op jit(solution)/shard_map/ppermute | solution.py:28
  124.2 13.3 %collective-permute-start.2 = (bf16[4,2,2,2,4096]{4,3,2,0,1:T(2,128)(2,1)S(1)}, bf16[4,2,2,2,4096]{4,3,2,0,1:T(2,128)(2,1)S(1)}, u32[]{:S(2)}, u32[]{:S(2)}) collective-permute-start(bf16[4,2,2,2,4096]{4,3,2,0,1:T(2,128)(2,1)S(1)} %get-tuple-element.22), channel_id=1, source_target_pairs={{1,0},{2,1},{3,2},{4,3},{5,4},{6,5},{7,6},{9,8},{10,9},{11,10},{12... | collective-permute-start | bytes 786440 | tf_op jit(solution)/shard_map/ppermute | solution.py:31
  148.0 8.3 %collective-permute-start.3 = (bf16[16,2,1,4096]{3,0,2,1:T(8,128)(2,1)S(1)}, bf16[16,2,1,4096]{3,0,2,1:T(8,128)(2,1)S(1)}, u32[]{:S(2)}, u32[]{:S(2)}) collective-permute-start(bf16[16,2,1,4096]{3,0,2,1:T(8,128)(2,1)S(1)} %get-tuple-element.20), channel_id=1, source_target_pairs={{0,16},{16,0},{8,24},{24,8},{1,17},{17,1},{9,25},{25,9},{2,18},{18... | collective-permute-start | bytes 786440 | tf_op jit(solution)/shard_map/ppermute | solution.py:20
  156.4 7.8 %collective-permute-start.4 = (bf16[4,2,2,1,4096]{4,0,2,3,1:T(4,128)(2,1)S(1)}, bf16[4,2,2,1,4096]{4,0,2,3,1:T(4,128)(2,1)S(1)}, u32[]{:S(2)}, u32[]{:S(2)}) collective-permute-start(bf16[4,2,2,1,4096]{4,0,2,3,1:T(4,128)(2,1)S(1)} %get-tuple-element.17), channel_id=1, source_target_pairs={{0,1},{1,2},{2,3},{3,4},{4,5},{5,6},{6,7},{8,9},{9,10},{10,11},{11... | collective-permute-start | bytes 393224 | tf_op jit(solution)/shard_map/ppermute | solution.py:28
  158.3 8.2 %collective-permute-start.5 = (bf16[4,2,2,1,4096]{4,0,2,3,1:T(4,128)(2,1)S(1)}, bf16[4,2,2,1,4096]{4,0,2,3,1:T(4,128)(2,1)S(1)}, u32[]{:S(2)}, u32[]{:S(2)}) collective-permute-start(bf16[4,2,2,1,4096]{4,0,2,3,1:T(4,128)(2,1)S(1)} %get-tuple-element.18), channel_id=1, source_target_pairs={{1,0},{2,1},{3,2},{4,3},{5,4},{6,5},{7,6},{9,8},{10,9},{11,10},{12... | collective-permute-start | bytes 393224 | tf_op jit(solution)/shard_map/ppermute | solution.py:31
Sparse Core Ops, SparseCore 0:
  23.9 89.6 reduce-scatter.3

commit v2 on v1

--- a/solution.py
+++ b/solution.py
@@ -1,13 +1,18 @@
+import functools
 import math
 
 import jax
 import jax.numpy as jnp
 from jax import lax
+from jax.experimental import pallas as pl
+from jax.experimental.pallas import tpu as pltpu
 from jax.sharding import PartitionSpec as P
 
 NR = 16384
 RADIX = 128
 BAND = 8
+CHUNKS = 8
+MESH = pl.DeviceIdType.MESH
 
 
 def from_partner(block, axis, bit):
@@ -88,6 +93,98 @@
 
 def beam_term(weights, pulses):
     return jnp.einsum("kspq,pqr->ksr", weights, pulses, preferred_element_type=jnp.float32)
+
+
+def reduce_kernel(
+    beam_count, comp_count, part_ref, out_ref, recv_one, send_two, recv_two,
+    one_send, one_recv, two_send, two_recv,
+):
+    z = lax.axis_index("beam")
+    y = lax.axis_index("comp")
+    width = part_ref.shape[-1] // CHUNKS
+    barrier = pltpu.get_barrier_semaphore()
+    for d in range(1, comp_count):
+        pl.semaphore_signal(
+            barrier, inc=1, device_id={"comp": lax.rem(y + d, comp_count)}, device_id_type=MESH
+        )
+    for d in range(1, beam_count):
+        pl.semaphore_signal(
+            barrier, inc=1, device_id={"beam": lax.rem(z + d, beam_count)}, device_id_type=MESH
+        )
+    pl.semaphore_wait(barrier, comp_count + beam_count - 2)
+    first = []
+    for j in range(CHUNKS):
+        cols = pl.ds(j * width, width)
+        for d in range(1, comp_count):
+            peer = lax.rem(y + d, comp_count)
+            copy = pltpu.make_async_remote_copy(
+                src_ref=part_ref.at[:, peer, :, cols],
+                dst_ref=recv_one.at[d - 1, :, :, cols],
+                send_sem=one_send.at[d - 1, j],
+                recv_sem=one_recv.at[d - 1, j],
+                device_id={"comp": peer},
+                device_id_type=MESH,
+            )
+            copy.start()
+            first.append(copy)
+    second = []
+    for j in range(CHUNKS):
+        cols = pl.ds(j * width, width)
+        for copy in first[j * (comp_count - 1) : (j + 1) * (comp_count - 1)]:
+            copy.wait_recv()
+        total = part_ref[:, y, :, cols].astype(jnp.float32)
+        for d in range(1, comp_count):
+            total += recv_one[d - 1, :, :, cols].astype(jnp.float32)
+        send_two[:, :, cols] = total.astype(jnp.bfloat16)
+        for d in range(1, beam_count):
+            peer = lax.rem(z + d, beam_count)
+            copy = pltpu.make_async_remote_copy(
+                src_ref=send_two.at[peer, :, cols],
+                dst_ref=recv_two.at[d - 1, :, cols],
+                send_sem=two_send.at[d - 1, j],
+                recv_sem=two_recv.at[d - 1, j],
+                device_id={"beam": peer},
+                device_id_type=MESH,
+            )
+            copy.start()
+            second.append(copy)
+    for j in range(CHUNKS):
+        cols = pl.ds(j * width, width)
+        for copy in second[j * (beam_count - 1) : (j + 1) * (beam_count - 1)]:
+            copy.wait_recv()
+        total = part_ref[z, y, :, cols].astype(jnp.float32)
+        for d in range(1, comp_count):
+            total += recv_one[d - 1, z, :, cols].astype(jnp.float32)
+        for d in range(1, beam_count):
+            total += recv_two[d - 1, :, cols].astype(jnp.float32)
+        out_ref[:, cols] = total
+    for copy in first + second:
+        copy.wait_send()
+
+
+def reduce_beams(partial, beam_count, comp_count):
+    blocks = beam_count * comp_count
+    rows = partial.shape[0] // blocks
+    length = partial.size // partial.shape[0]
+    part = partial.reshape(beam_count, comp_count, rows, length)
+    return pl.pallas_call(
+        functools.partial(reduce_kernel, beam_count, comp_count),
+        out_shape=jax.ShapeDtypeStruct((rows, length), jnp.float32),
+        in_specs=[pl.BlockSpec(memory_space=pltpu.VMEM)],
+        out_specs=pl.BlockSpec(memory_space=pltpu.VMEM),
+        scratch_shapes=[
+            pltpu.VMEM((comp_count - 1, beam_count, rows, length), jnp.bfloat16),
+            pltpu.VMEM((beam_count, rows, length), jnp.bfloat16),
+            pltpu.VMEM((beam_count - 1, rows, length), jnp.bfloat16),
+            pltpu.SemaphoreType.DMA((comp_count - 1, CHUNKS)),
+            pltpu.SemaphoreType.DMA((comp_count - 1, CHUNKS)),
+            pltpu.SemaphoreType.DMA((beam_count - 1, CHUNKS)),
+            pltpu.SemaphoreType.DMA((beam_count - 1, CHUNKS)),
+        ],
+        compiler_params=pltpu.CompilerParams(
+            collective_id=0, has_side_effects=True, vmem_limit_bytes=56 * 2**20
+        ),
+    )(part)
 
 
 def band_matrix(offset, weight, span):
@@ -129,8 +226,8 @@
     levels = sub_count.bit_length() - 1
     sub_index = lax.axis_index("sub")
     partial = beam_term(weights, raw_pulses).astype(jnp.bfloat16)
-    summed = lax.psum_scatter(partial, ("beam", "comp"), scatter_dimension=0, tiled=True)
-    subimage = compress(summed, range_filter)
+    summed = reduce_beams(partial, beam_devices, comp_devices)
+    subimage = compress(summed.astype(jnp.bfloat16), range_filter)
     margin = BAND // 2
     block_rows = NR // sub_count
     beam_count = first_beams

time: 184 us -> 153 us (0.83)
  waiting for transfers between devices: 109 us -> 20.3 us
  Pallas kernels: 0 us -> 59.3 us
  between operations: 13.8 us -> 0.47 us
  local copies, waits for them, and re-layouts: 11.7 us -> 21.7 us
    unnamed x2 -> x0, waiting for transfers between devices: 88.1 us -> none
    pallas_call x0 -> x1, Pallas kernels: none -> 59.3 us  [reduce_beams(): pl.pallas_call(functools.partial(reduce_kernel, beam_count, comp_count),...]
    reshape x1, local copies, waits for them, and re-layouts: 0.39 us -> 8.14 us  [reduce_beams(): part = partial.reshape(beam_count, comp_count, rows, length)]
    convert_element_type x0 -> x1, local copies, waits for them, and re-layouts: none -> 6.5 us  [body(): partial = beam_term(weights, raw_pulses).astype(jnp.bfloat16)]
    unnamed x10 -> x9, local copies, waits for them, and re-layouts: 2.63 us -> 0.3 us
  transfers between devices with their start and end apart: 7 -> 6, of which waited for: 7 -> 6; matrix products, arithmetic and copies ran while one was open for 1% -> 1% of each run, Pallas kernels for 0% -> 0%
where the time goes in v2:
time: 153 us; the launch traced here: 152 us
  Pallas kernels  59.3 us (39%)
  local copies, waits for them, and re-layouts  21.7 us (14%)
  waiting for transfers between devices  20.3 us (13%)
  matrix products  18.1 us (12%)
  other arithmetic  16.1 us (11%)
  starting transfers between devices  15.6 us (10%)
    pallas_call x1, Pallas kernels, reduce_beams(): pl.pallas_call(functools.partial(reduce_kernel, beam_count, comp_count),...  59.3 us
    dot_general x1, matrix products, beam_term(): jnp.einsum('kspq,pqr->ksr', weights, pulses, preferred_element_type=jnp.f...  13.1 us
    ppermute x2, starting transfers between devices, with_halo(): lax.ppermute(lax.slice_in_dim(block, 0, width, axis=dim), axis, backward)  9.57 us
    reshape x1, local copies, waits for them, and re-layouts, reduce_beams(): part = partial.reshape(beam_count, comp_count, rows, length)  8.14 us
    ppermute x2, waiting for transfers between devices, with_halo(): lax.ppermute(lax.slice_in_dim(block, block.shape[dim] - width, None, axis...  7.65 us
    ppermute x2, waiting for transfers between devices, from_partner(): return lax.ppermute(block, axis, route)  7.47 us
    convert_element_type x1, local copies, waits for them, and re-layouts, body(): partial = beam_term(weights, raw_pulses).astype(jnp.bfloat16)  6.5 us
    ppermute x2, waiting for transfers between devices, with_halo(): lax.ppermute(lax.slice_in_dim(block, 0, width, axis=dim), axis, backward)  5.21 us
  transfers between devices with their start and end apart: 6, of which 6 were waited for; matrix products, arithmetic and copies ran while one was open for 1% of the time, Pallas kernels for 0%

profile of v2, /device:TPU:8, one launch (start us, length us, event | category | flops | bytes accessed | tf_op | source)
XLA Modules:
  0.0 151.6 jit_solution(16504368887001364593)
XLA Ops:
  0.0 0.9 fusion.77
  0.9 0.9 negate_bitcast_fusion
  1.8 0.3 negate_convert_fusion
  2.1 0.3 fusion.72
  2.3 0.3 fusion.70
  2.6 0.3 sine_negate_fusion
  2.9 13.1 %fusion = bf16[64,2,16384]{2,0,1:T(8,128)(2,1)S(1)} fusion(bf16[128,2,16384]{2,1,0:T(2,128)(2,1)} %param.6, bf16[64,1,128,2]{2,0,3,1:T(8,128)(2,1)S(1)} %get-tuple-element.30, bf16[64,1,128,2]{2,0,3,1:T(8,128)(2,1)S(1)} %get-tuple-element.29), kind=kOutput, calls=%fused_computation.1 | convolution fusion | flops 1075871744 | bytes 12648448 | tf_op jit(solution)/shard_map/kspq,pqr->ksr/dot_general | solution.py:95
  16.0 6.5 %copy.43 = bf16[64,2,16384]{2,1,0:T(2,128)(2,1)} copy(bf16[64,2,16384]{2,0,1:T(8,128)(2,1)S(1)} %fusion) | data formatting | bytes 8388608 | tf_op jit(solution)/shard_map/convert_element_type | solution.py:228
  22.5 8.1 %reshape.541.part_ref = bf16[4,2,8,32768]{3,2,1,0:T(8,128)(2,1)} reshape(bf16[64,2,16384]{2,1,0:T(2,128)(2,1)} %copy.43) | data formatting | bytes 8388608 | tf_op jit(solution)/shard_map/reshape | solution.py:169
  30.6 59.3 %shard_map.64 = f32[8,32768]{1,0:T(8,128)} custom-call(bf16[4,2,8,32768]{3,2,1,0:T(8,128)(2,1)} %reshape.541.part_ref), custom_call_target="tpu_custom_call" | custom-call | tf_op jit(solution)/shard_map/pallas_call | solution.py:170
  90.0 1.3 convert_bitcast_fusion
  91.3 0.3 convolution_bitcast_fusion.5
  91.8 0.1 subtract_bitcast_fusion
  92.0 0.3 convolution_bitcast_fusion.3
  92.4 0.3 fusion.4
  92.7 0.2 reshape.543
  93.0 0.2 multiply_convert_fusion
  93.2 0.3 copy_dynamic-update-slice_fusion.1
  93.5 0.3 copy_dynamic-update-slice_fusion
  93.8 0.4 dynamic-slice_bitcast_fusion.1
  95.0 0.8 collective-permute-done
  95.8 0.8 fusion.49
  96.6 2.5 %collective-permute-start.1 = (bf16[4,2,2,2,4096]{4,3,2,0,1:T(2,128)(2,1)S(1)}, bf16[4,2,2,2,4096]{4,3,2,0,1:T(2,128)(2,1)S(1)}, u32[]{:S(2)}, u32[]{:S(2)}) collective-permute-start(bf16[4,2,2,2,4096]{4,3,2,0,1:T(2,128)(2,1)S(1)} %get-tuple-element.21), channel_id=1, source_target_pairs={{0,1},{1,2},{2,3},{3,4},{4,5},{5,6},{6,7},{8,9},{9,10},{10,11},{11... | collective-permute-start | bytes 786440 | tf_op jit(solution)/shard_map/ppermute | solution.py:33
  99.0 4.5 %collective-permute-start.2 = (bf16[4,2,2,2,4096]{4,3,2,0,1:T(2,128)(2,1)S(1)}, bf16[4,2,2,2,4096]{4,3,2,0,1:T(2,128)(2,1)S(1)}, u32[]{:S(2)}, u32[]{:S(2)}) collective-permute-start(bf16[4,2,2,2,4096]{4,3,2,0,1:T(2,128)(2,1)S(1)} %get-tuple-element.22), channel_id=1, source_target_pairs={{1,0},{2,1},{3,2},{4,3},{5,4},{6,5},{7,6},{9,8},{10,9},{11,10},{12... | collective-permute-start | bytes 786440 | tf_op jit(solution)/shard_map/ppermute | solution.py:36
  103.6 6.9 %collective-permute-done.1 = bf16[4,2,2,2,4096]{4,3,2,0,1:T(2,128)(2,1)S(1)} collective-permute-done((bf16[4,2,2,2,4096]{4,3,2,0,1:T(2,128)(2,1)S(1)}, bf16[4,2,2,2,4096]{4,3,2,0,1:T(2,128)(2,1)S(1)}, u32[]{:S(2)}, u32[]{:S(2)}) %collective-permute-start.1) | collective-permute-done | bytes 262176 | tf_op jit(solution)/shard_map/ppermute | solution.py:33
  110.5 2.8 %collective-permute-done.2 = bf16[4,2,2,2,4096]{4,3,2,0,1:T(2,128)(2,1)S(1)} collective-permute-done((bf16[4,2,2,2,4096]{4,3,2,0,1:T(2,128)(2,1)S(1)}, bf16[4,2,2,2,4096]{4,3,2,0,1:T(2,128)(2,1)S(1)}, u32[]{:S(2)}, u32[]{:S(2)}) %collective-permute-start.2) | collective-permute-done | bytes 262176 | tf_op jit(solution)/shard_map/ppermute | solution.py:36
  113.3 1.6 %pad_maximum_fusion.1 = bf16[16,2,2,2,4096]{4,3,2,0,1:T(2,128)(2,1)S(1)} fusion(bf16[4,2,2,2,4096]{4,3,2,0,1:T(2,128)(2,1)S(1)} %collective-permute-done.2, bf16[8,1,2,2,4096]{4,3,2,0,1:T(2,128)(2,1)S(1)} %bitcast.163, bf16[8,1,2,2,4096]{4,3,2,0,1:T(2,128)(2,1)S(1)} %get-tuple-element.23, bf16[4,2,2,2,4096]{4,3,2,0,1:T(2,128)(2,1)S(1)} %collective-permute-done.1), kind=kLoop, calls=%fused_computation.12 | loop fusion | flops 1572864 | bytes 2097152 | tf_op jit(solution)/shard_map/concatenate | solution.py:37
  115.0 0.9 fusion.95
  115.9 0.4 reshape_squeeze.12
  116.3 0.4 dot_general.45
  116.7 0.4 reshape_squeeze.13
  117.1 0.4 dot_general.48
  117.5 1.0 fusion.40
  118.5 1.0 fusion.38
  119.5 4.2 %fusion.31 = (bf16[16,1,2,4096]{3,0,2,1:T(8,128)(2,1)S(1)}, bf16[16,1,2,4096]{3,0,2,1:T(8,128)(2,1)S(1)}) fusion(f32[16,2,2,4096]{3,0,2,1:T(8,128)S(1)} %fusion.38, f32[16,2,2,4096]{3,0,2,1:T(8,128)S(1)} %fusion.40, f32[16]{0:T(128)S(1)} %get-tuple-element.40, f32[2,4096]{1,0:T(2,128)S(1)} %multiply_add_fusion, f32[16]{0:T(128)S(1)} %get-tuple-element.39), kind=kLoop, calls=%fused_computation.54 | loop fusion | flops 2359296 | bytes 2654336 | tf_op jit(solution)/shard_map/convert.1
  123.7 1.5 %collective-permute-start.3 = (bf16[16,2,1,4096]{3,0,2,1:T(8,128)(2,1)S(1)}, bf16[16,2,1,4096]{3,0,2,1:T(8,128)(2,1)S(1)}, u32[]{:S(2)}, u32[]{:S(2)}) collective-permute-start(bf16[16,2,1,4096]{3,0,2,1:T(8,128)(2,1)S(1)} %get-tuple-element.20), channel_id=1, source_target_pairs={{0,16},{16,0},{8,24},{24,8},{1,17},{17,1},{9,25},{25,9},{2,18},{18... | collective-permute-start | bytes 786440 | tf_op jit(solution)/shard_map/ppermute | solution.py:25
  125.4 6.7 %collective-permute-done.3 = bf16[16,2,1,4096]{3,0,2,1:T(8,128)(2,1)S(1)} collective-permute-done((bf16[16,2,1,4096]{3,0,2,1:T(8,128)(2,1)S(1)}, bf16[16,2,1,4096]{3,0,2,1:T(8,128)(2,1)S(1)}, u32[]{:S(2)}, u32[]{:S(2)}) %collective-permute-start.3) | collective-permute-done | bytes 262176 | tf_op jit(solution)/shard_map/ppermute | solution.py:25
  132.1 1.9 %collective-permute-start.4 = (bf16[4,2,2,1,4096]{4,0,2,3,1:T(4,128)(2,1)S(1)}, bf16[4,2,2,1,4096]{4,0,2,3,1:T(4,128)(2,1)S(1)}, u32[]{:S(2)}, u32[]{:S(2)}) collective-permute-start(bf16[4,2,2,1,4096]{4,0,2,3,1:T(4,128)(2,1)S(1)} %get-tuple-element.17), channel_id=1, source_target_pairs={{0,1},{1,2},{2,3},{3,4},{4,5},{5,6},{6,7},{8,9},{9,10},{10,11},{11... | collective-permute-start | bytes 393224 | tf_op jit(solution)/shard_map/ppermute | solution.py:33
  134.1 5.1 %collective-permute-start.5 = (bf16[4,2,2,1,4096]{4,0,2,3,1:T(4,128)(2,1)S(1)}, bf16[4,2,2,1,4096]{4,0,2,3,1:T(4,128)(2,1)S(1)}, u32[]{:S(2)}, u32[]{:S(2)}) collective-permute-start(bf16[4,2,2,1,4096]{4,0,2,3,1:T(4,128)(2,1)S(1)} %get-tuple-element.18), channel_id=1, source_target_pairs={{1,0},{2,1},{3,2},{4,3},{5,4},{6,5},{7,6},{9,8},{10,9},{11,10},{12... | collective-permute-start | bytes 393224 | tf_op jit(solution)/shard_map/ppermute | solution.py:36
  139.2 0.8 collective-permute-done.4
  140.0 2.4 %collective-permute-done.5 = bf16[4,2,2,1,4096]{4,0,2,3,1:T(4,128)(2,1)S(1)} collective-permute-done((bf16[4,2,2,1,4096]{4,0,2,3,1:T(4,128)(2,1)S(1)}, bf16[4,2,2,1,4096]{4,0,2,3,1:T(4,128)(2,1)S(1)}, u32[]{:S(2)}, u32[]{:S(2)}) %collective-permute-start.5) | collective-permute-done | bytes 131104 | tf_op jit(solution)/shard_map/ppermute | solution.py:36
  142.4 0.3 pad_maximum_fusion.2
  142.8 0.4 copy.56
  143.2 0.4 copy.58
  143.6 1.0 convolution_bitcast_fusion.2
  144.6 1.0 convolution_bitcast_fusion.1
  145.6 4.1 %fusion.23 = (f32[32,1,1,4096]{3,0,1,2:T(8,128)S(1)}, f32[32,1,1,4096]{3,0,1,2:T(8,128)S(1)}) fusion(f32[32,2,1,4096]{3,0,1,2:T(8,128)S(1)} %convolution_bitcast_fusion.1, f32[32,2,1,4096]{3,0,1,2:T(8,128)S(1)} %convolution_bitcast_fusion.2, f32[32]{0:T(128)S(1)} %get-tuple-element.36, f32[4096]{0:T(1024)S(1)} %multiply_add_fusion.1, f32[32]{0:T(128)S(1)} %get-tuple-element.35), kind=kLoop, calls=%fused_computation.46 | loop fusion | flops 2097152 | bytes 3162368 | tf_op jit(solution)/shard_map/add | solution.py:274
  149.8 1.8 %copy.60 = f32[32,2,4096]{2,1,0:T(2,128)} copy(f32[32,2,4096]{2,0,1:T(8,128)S(1)} %maximum_bitcast_fusion) | data formatting | bytes 2097152 | tf_op jit(solution)/shard_map/reshape | solution.py:276
  (39 shorter events, 1.6 us)
Async XLA Ops:
  92.0 0.9 copy-start
  92.3 2.0 %copy-start.2 = (s32[2,48]{1,0:T(2,128)S(1)}, s32[2,48]{1,0:T(2,128)}, u32[]{:S(2)}) copy-start(s32[2,48]{1,0:T(2,128)} %param.9) | copy-start | bytes 1156
  92.3 2.0 %copy-start.1 = (f32[2,48,8]{1,2,0:T(8,128)S(1)}, f32[2,48,8]{1,2,0:T(8,128)}, u32[]{:S(2)}) copy-start(f32[2,48,8]{1,2,0:T(8,128)} %param.10) | copy-start | bytes 9220
  92.4 2.2 %copy-start.3 = (f32[2,48]{1,0:T(2,128)S(1)}, f32[2,48]{1,0:T(2,128)}, u32[]{:S(2)}) copy-start(f32[2,48]{1,0:T(2,128)} %param.11) | copy-start | bytes 1156
  94.2 1.6 %collective-permute-start = (bf16[8,2,2,4096]{3,2,1,0:T(2,128)(2,1)S(1)}, bf16[8,2,2,4096]{3,2,1,0:T(2,128)(2,1)S(1)}, u32[]{:S(2)}, u32[]{:S(2)}) collective-permute-start(bf16[8,2,2,4096]{3,2,1,0:T(2,128)(2,1)S(1)} %get-tuple-element.24), channel_id=1, source_target_pairs={{0,8},{8,0},{16,24},{24,16},{1,9},{9,1},{17,25},{25,17},{2,10},{10... | collective-permute-start | bytes 786440 | tf_op jit(solution)/shard_map/ppermute | solution.py:25
  96.6 13.9 %collective-permute-start.1 = (bf16[4,2,2,2,4096]{4,3,2,0,1:T(2,128)(2,1)S(1)}, bf16[4,2,2,2,4096]{4,3,2,0,1:T(2,128)(2,1)S(1)}, u32[]{:S(2)}, u32[]{:S(2)}) collective-permute-start(bf16[4,2,2,2,4096]{4,3,2,0,1:T(2,128)(2,1)S(1)} %get-tuple-element.21), channel_id=1, source_target_pairs={{0,1},{1,2},{2,3},{3,4},{4,5},{5,6},{6,7},{8,9},{9,10},{10,11},{11... | collective-permute-start | bytes 786440 | tf_op jit(solution)/shard_map/ppermute | solution.py:33
  99.0 14.3 %collective-permute-start.2 = (bf16[4,2,2,2,4096]{4,3,2,0,1:T(2,128)(2,1)S(1)}, bf16[4,2,2,2,4096]{4,3,2,0,1:T(2,128)(2,1)S(1)}, u32[]{:S(2)}, u32[]{:S(2)}) collective-permute-start(bf16[4,2,2,2,4096]{4,3,2,0,1:T(2,128)(2,1)S(1)} %get-tuple-element.22), channel_id=1, source_target_pairs={{1,0},{2,1},{3,2},{4,3},{5,4},{6,5},{7,6},{9,8},{10,9},{11,10},{12... | collective-permute-start | bytes 786440 | tf_op jit(solution)/shard_map/ppermute | solution.py:36
  123.7 8.3 %collective-permute-start.3 = (bf16[16,2,1,4096]{3,0,2,1:T(8,128)(2,1)S(1)}, bf16[16,2,1,4096]{3,0,2,1:T(8,128)(2,1)S(1)}, u32[]{:S(2)}, u32[]{:S(2)}) collective-permute-start(bf16[16,2,1,4096]{3,0,2,1:T(8,128)(2,1)S(1)} %get-tuple-element.20), channel_id=1, source_target_pairs={{0,16},{16,0},{8,24},{24,8},{1,17},{17,1},{9,25},{25,9},{2,18},{18... | collective-permute-start | bytes 786440 | tf_op jit(solution)/shard_map/ppermute | solution.py:25
  132.1 7.9 %collective-permute-start.4 = (bf16[4,2,2,1,4096]{4,0,2,3,1:T(4,128)(2,1)S(1)}, bf16[4,2,2,1,4096]{4,0,2,3,1:T(4,128)(2,1)S(1)}, u32[]{:S(2)}, u32[]{:S(2)}) collective-permute-start(bf16[4,2,2,1,4096]{4,0,2,3,1:T(4,128)(2,1)S(1)} %get-tuple-element.17), channel_id=1, source_target_pairs={{0,1},{1,2},{2,3},{3,4},{4,5},{5,6},{6,7},{8,9},{9,10},{10,11},{11... | collective-permute-start | bytes 393224 | tf_op jit(solution)/shard_map/ppermute | solution.py:33
  134.1 8.3 %collective-permute-start.5 = (bf16[4,2,2,1,4096]{4,0,2,3,1:T(4,128)(2,1)S(1)}, bf16[4,2,2,1,4096]{4,0,2,3,1:T(4,128)(2,1)S(1)}, u32[]{:S(2)}, u32[]{:S(2)}) collective-permute-start(bf16[4,2,2,1,4096]{4,0,2,3,1:T(4,128)(2,1)S(1)} %get-tuple-element.18), channel_id=1, source_target_pairs={{1,0},{2,1},{3,2},{4,3},{5,4},{6,5},{7,6},{9,8},{10,9},{11,10},{12... | collective-permute-start | bytes 393224 | tf_op jit(solution)/shard_map/ppermute | solution.py:36

commit v3 on v2

v3 whole, which is shorter than its diff:
```python
import functools
import math

import jax
import jax.numpy as jnp
from jax import lax
from jax.experimental import pallas as pl
from jax.experimental.pallas import tpu as pltpu
from jax.sharding import PartitionSpec as P

NR = 16384
RADIX = 128
BAND = 8
CHUNKS = 8
MESH = pl.DeviceIdType.MESH


def dft_table(length):
    index_row = jnp.arange(length, dtype=jnp.int32)
    product = index_row[:, None] * index_row[None, :] % length
    phase_angle = product.astype(jnp.float32) * (2.0 * math.pi / length)
    return (jnp.cos(phase_angle).astype(jnp.bfloat16), (-jnp.sin(phase_angle)).astype(jnp.bfloat16))


def real_form(length):
    cos_part, sin_part = dft_table(length)
    upper_rows = jnp.concatenate([cos_part, sin_part], axis=1)
    lower_rows = jnp.concatenate([-sin_part, cos_part], axis=1)
    return jnp.concatenate([upper_rows, lower_rows], axis=0)


def twiddle():
    freq_index = jnp.arange(RADIX, dtype=jnp.int32)[:, None]
    time_index = jnp.arange(RADIX, dtype=jnp.int32)[None, :]
    phase_angle = (freq_index * time_index % NR).astype(jnp.float32) * (2.0 * math.pi / NR)
    return (jnp.cos(phase_angle), -jnp.sin(phase_angle))


def compress(beams, range_filter):
    number = beams.shape[1]
    samples = beams.reshape(2, number, RADIX, RADIX)
    first = real_form(RADIX).reshape(2, RADIX, 2, RADIX)
    section_one = jnp.einsum("rpan,rask->spkn", samples, first, preferred_element_type=jnp.float32)
    cos_part, sin_part = twiddle()
    real_in = section_one[0]
    imag_in = section_one[1]
    turned = jnp.stack(
        [real_in * cos_part - imag_in * sin_part, real_in * sin_part + imag_in * cos_part], 0
    )
    high = turned.astype(jnp.bfloat16)
    low = (turned - high.astype(jnp.float32)).astype(jnp.bfloat16)
    spectrum = jnp.einsum("rpkn,rnsm->spmk", high, first, preferred_element_type=jnp.float32)
    spectrum += jnp.einsum("rpkn,rnsm->spmk", low, first, preferred_element_type=jnp.float32)
    spectrum = spectrum.reshape(2, number, NR)
    factor = NR ** (-0.5)
    real_out = (spectrum[0] * range_filter[0] - spectrum[1] * range_filter[1]) * factor
    imag_out = (spectrum[0] * range_filter[1] + spectrum[1] * range_filter[0]) * factor
    return jnp.stack([real_out, imag_out], 0)


def steering(phase_angle, factor):
    real_part = (jnp.cos(phase_angle) * factor).astype(jnp.bfloat16)
    imag_part = (jnp.sin(phase_angle) * factor).astype(jnp.bfloat16)
    return jnp.stack(
        [jnp.stack([real_part, -imag_part], -1), jnp.stack([imag_part, real_part], -1)], 1
    )


def beam_term(weights, pulses):
    return jnp.einsum("kspq,pqr->skr", weights, pulses, preferred_element_type=jnp.float32)


def reduce_kernel(
    beam_count, comp_count, part_ref, out_ref, recv_one, send_two, recv_two,
    one_send, one_recv, two_send, two_recv,
):
    z = lax.axis_index("beam")
    y = lax.axis_index("comp")
    width = part_ref.shape[-1] // CHUNKS
    barrier = pltpu.get_barrier_semaphore()
    for d in range(1, comp_count):
        pl.semaphore_signal(
            barrier, inc=1, device_id={"comp": lax.rem(y + d, comp_count)}, device_id_type=MESH
        )
    for d in range(1, beam_count):
        pl.semaphore_signal(
            barrier, inc=1, device_id={"beam": lax.rem(z + d, beam_count)}, device_id_type=MESH
        )
    pl.semaphore_wait(barrier, comp_count + beam_count - 2)
    first = []
    for j in range(CHUNKS):
        cols = pl.ds(j * width, width)
        for d in range(1, comp_count):
            peer = lax.rem(y + d, comp_count)
            copy = pltpu.make_async_remote_copy(
                src_ref=part_ref.at[:, :, peer, :, cols],
                dst_ref=recv_one.at[d - 1, :, :, :, cols],
                send_sem=one_send.at[d - 1, j],
                recv_sem=one_recv.at[d - 1, j],
                device_id={"comp": peer},
                device_id_type=MESH,
            )
            copy.start()
            first.append(copy)
    second = []
    for j in range(CHUNKS):
        cols = pl.ds(j * width, width)
        for copy in first[j * (comp_count - 1) : (j + 1) * (comp_count - 1)]:
            copy.wait_recv()
        total = part_ref[:, :, y, :, cols].astype(jnp.float32)
        for d in range(1, comp_count):
            total += recv_one[d - 1, :, :, :, cols].astype(jnp.float32)
        send_two[:, :, :, cols] = total.astype(jnp.bfloat16)
        for d in range(1, beam_count):
            peer = lax.rem(z + d, beam_count)
            copy = pltpu.make_async_remote_copy(
                src_ref=send_two.at[:, peer, :, cols],
                dst_ref=recv_two.at[d - 1, :, :, cols],
                send_sem=two_send.at[d - 1, j],
                recv_sem=two_recv.at[d - 1, j],
                device_id={"beam": peer},
                device_id_type=MESH,
            )
            copy.start()
            second.append(copy)
    for j in range(CHUNKS):
        cols = pl.ds(j * width, width)
        for copy in second[j * (beam_count - 1) : (j + 1) * (beam_count - 1)]:
            copy.wait_recv()
        total = part_ref[:, z, y, :, cols].astype(jnp.float32)
        for d in range(1, comp_count):
            total += recv_one[d - 1, :, z, :, cols].astype(jnp.float32)
        for d in range(1, beam_count):
            total += recv_two[d - 1, :, :, cols].astype(jnp.float32)
        out_ref[:, :, cols] = total.astype(jnp.bfloat16)
    for copy in first + second:
        copy.wait_send()


def reduce_beams(partial, beam_count, comp_count):
    blocks = beam_count * comp_count
    rows = partial.shape[1] // blocks
    length = partial.shape[2]
    part = partial.reshape(2, beam_count, comp_count, rows, length)
    return pl.pallas_call(
        functools.partial(reduce_kernel, beam_count, comp_count),
        out_shape=jax.ShapeDtypeStruct((2, rows, length), jnp.bfloat16),
        in_specs=[pl.BlockSpec(memory_space=pltpu.VMEM)],
        out_specs=pl.BlockSpec(memory_space=pltpu.VMEM),
        scratch_shapes=[
            pltpu.VMEM((comp_count - 1, 2, beam_count, rows, length), jnp.bfloat16),
            pltpu.VMEM((2, beam_count, rows, length), jnp.bfloat16),
            pltpu.VMEM((beam_count - 1, 2, rows, length), jnp.bfloat16),
            pltpu.SemaphoreType.DMA((comp_count - 1, CHUNKS)),
            pltpu.SemaphoreType.DMA((comp_count - 1, CHUNKS)),
            pltpu.SemaphoreType.DMA((beam_count - 1, CHUNKS)),
            pltpu.SemaphoreType.DMA((beam_count - 1, CHUNKS)),
        ],
        compiler_params=pltpu.CompilerParams(
            collective_id=0, has_side_effects=True, vmem_limit_bytes=56 * 2**20
        ),
    )(part)


def band_matrix(offset, weight, span):
    tap_index = offset[:, None] + BAND // 2 + jnp.arange(BAND, dtype=jnp.int32)[None, :]
    matches = tap_index[:, :, None] == jnp.arange(span, dtype=jnp.int32)[None, None, :]
    return jnp.sum(
        jnp.where(matches, weight[:, :, None], jnp.zeros_like(weight)[:, :, None]), axis=1
    )


def exchange_kernel(
    counts, spread, image_ref, out_ref, send_sem, recv_sem, low_send, low_recv, high_send,
    high_recv, own_sem,
):
    sub_count, beam_count, comp_count = counts
    s = lax.axis_index("sub")
    block = lax.axis_index("beam") * comp_count + lax.axis_index("comp")
    has_low = block > 0
    has_high = block < beam_count * comp_count - 1
    width = out_ref.shape[-1]
    hops = sub_count if spread else 1

    def place(d, step):
        target = block + step
        return {
            "sub": lax.rem(s + d, sub_count),
            "beam": lax.div(target, comp_count),
            "comp": lax.rem(target, comp_count),
        }

    def columns(d):
        if not spread:
            return pl.ds(0, width)
        return pl.ds(pl.multiple_of(lax.rem(s + d, sub_count) * width, 128), width)

    barrier = pltpu.get_barrier_semaphore()
    for d in range(1, hops):
        pl.semaphore_signal(barrier, inc=1, device_id=place(d, 0), device_id_type=MESH)

    @pl.when(has_high)
    def _():
        for d in range(hops):
            pl.semaphore_signal(barrier, inc=1, device_id=place(d, 1), device_id_type=MESH)

    @pl.when(has_low)
    def _():
        for d in range(hops):
            pl.semaphore_signal(barrier, inc=1, device_id=place(d, -1), device_id_type=MESH)

    amount = hops - 1 + hops * (has_low.astype(jnp.int32) + has_high.astype(jnp.int32))
    pl.semaphore_wait(barrier, amount)

    def halo(d, step):
        source = slice(None) if not spread else s
        half = 1 if step > 0 else 0
        slot = 0 if step > 0 else out_ref.shape[2] - 1
        target = out_ref.at[:, :, slot] if not spread else out_ref.at[source, :, slot]
        origin = (
            image_ref.at[:, :, half]
            if not spread
            else image_ref.at[:, half, :, columns(d)]
        )
        return pltpu.make_async_remote_copy(
            src_ref=origin,
            dst_ref=target,
            send_sem=(low_send if step > 0 else high_send).at[d],
            recv_sem=(low_recv if step > 0 else high_recv).at[d],
            device_id=place(d, step),
            device_id_type=MESH,
        )

    @pl.when(has_high)
    def _():
        for d in range(hops):
            halo(d, 1).start()

    @pl.when(has_low)
    def _():
        for d in range(hops):
            halo(d, -1).start()

    copies = []
    for d in range(1, hops):
        copy = pltpu.make_async_remote_copy(
            src_ref=image_ref.at[:, :, :, columns(d)],
            dst_ref=out_ref.at[s, :, pl.ds(1, 2)],
            send_sem=send_sem.at[d],
            recv_sem=recv_sem.at[d],
            device_id=place(d, 0),
            device_id_type=MESH,
        )
        copy.start()
        copies.append(copy)
    if spread:
        own = pltpu.make_async_copy(
            image_ref.at[:, :, :, columns(0)], out_ref.at[s, :, pl.ds(1, 2)], own_sem
        )
        own.start()
        copies.append(own)

    low_slot = 0
    high_slot = out_ref.shape[2] - 1
    blank = jnp.zeros(out_ref.shape[:2] + out_ref.shape[3:], out_ref.dtype)

    @pl.when(has_low)
    def _():
        for d in range(hops):
            halo(d, 1).wait_recv()
            halo(d, -1).wait_send()

    @pl.when(jnp.logical_not(has_low))
    def _():
        out_ref[:, :, low_slot] = blank

    @pl.when(has_high)
    def _():
        for d in range(hops):
            halo(d, -1).wait_recv()
            halo(d, 1).wait_send()

    @pl.when(jnp.logical_not(has_high))
    def _():
        out_ref[:, :, high_slot] = blank

    for copy in copies:
        copy.wait()


def exchange(image, shape, counts, spread, kernel_id):
    hops = counts[0] if spread else 1
    return pl.pallas_call(
        functools.partial(exchange_kernel, counts, spread),
        out_shape=jax.ShapeDtypeStruct(shape, jnp.bfloat16),
        in_specs=[pl.BlockSpec(memory_space=pltpu.VMEM)],
        out_specs=pl.BlockSpec(memory_space=pltpu.VMEM),
        scratch_shapes=[pltpu.SemaphoreType.DMA((hops,))] * 6 + [pltpu.SemaphoreType.DMA],
        compiler_params=pltpu.CompilerParams(
            collective_id=kernel_id, has_side_effects=True, vmem_limit_bytes=24 * 2**20
        ),
    )(image)


def phases(delay, start, width):
    coarse_row = (start + RADIX * jnp.arange(width // RADIX, dtype=jnp.int32)).astype(jnp.float32)
    coarse = delay[..., None] * (1.0 + coarse_row / NR)
    fine = delay[..., None] * (jnp.arange(RADIX, dtype=jnp.float32) / NR)
    cos_one, sin_one = jnp.cos(coarse)[..., None], jnp.sin(coarse)[..., None]
    cos_two, sin_two = jnp.cos(fine)[..., None, :], jnp.sin(fine)[..., None, :]
    cosine = cos_one * cos_two - sin_one * sin_two
    sine = sin_one * cos_two + cos_one * sin_two
    shape = delay.shape + (width,)
    return cosine.reshape(shape), sine.reshape(shape)


def merge(window, offset, weight, cosine, sine):
    groups, span, width = window.shape[0] // 2, window.shape[2], window.shape[3]
    paired = window.reshape(groups, 2, 2, span, width)
    real_sum, imag_sum = 0.0, 0.0
    for c in range(2):
        matrix = band_matrix(offset[c], weight[c], span)
        high = matrix.astype(jnp.bfloat16)
        low = (matrix - high.astype(jnp.float32)).astype(jnp.bfloat16)
        both = jnp.concatenate([high, low], axis=0)
        blended = jnp.einsum(
            "jw,gpwr->gpjr", both, paired[:, c], preferred_element_type=jnp.float32
        )
        count = matrix.shape[0]
        blended = blended[:, :, :count] + blended[:, :, count:]
        real_sum += cosine[c] * blended[:, 0] - sine[c] * blended[:, 1]
        imag_sum += sine[c] * blended[:, 0] + cosine[c] * blended[:, 1]
    return real_sum, imag_sum


def body(raw_pulses, range_filter, steer_angle, band_offsets, band_weights, beam_delay):
    sub_count = lax.axis_size("sub")
    beam_devices = lax.axis_size("beam")
    comp_devices = lax.axis_size("comp")
    counts = (sub_count, beam_devices, comp_devices)
    blocks = beam_devices * comp_devices
    factor = float(raw_pulses.shape[0] * blocks) ** (-0.5)
    first_beams = steer_angle.shape[0] // blocks
    levels = sub_count.bit_length() - 1
    margin = BAND // 2
    width = NR // sub_count
    start = lax.axis_index("sub") * width
    cosine, sine = phases(beam_delay, start, width)
    weights = steering(steer_angle, factor)
    partial = beam_term(weights, raw_pulses).astype(jnp.bfloat16)
    summed = reduce_beams(partial, beam_devices, comp_devices)
    image = compress(summed, range_filter).astype(jnp.bfloat16)
    image = image.reshape(2, first_beams // margin, margin, NR)
    window = exchange(image, (sub_count, 2, 4, margin, width), counts, True, 1)
    window = window.reshape(sub_count, 2, 4 * margin, width)
    beam_count = first_beams
    for level_index in range(levels):
        base = first_beams * (2 ** (level_index + 1) - 2)
        cols = slice(base, base + 2 * beam_count)
        real, imag = merge(
            window, band_offsets[:, cols], band_weights[:, cols], cosine[:, cols], sine[:, cols]
        )
        beam_count *= 2
        if level_index + 1 < levels:
            image = jnp.stack([real, imag], 1).astype(jnp.bfloat16)
            groups = image.shape[0]
            ends = jnp.stack([image[:, :, :margin], image[:, :, -margin:]], 2)
            edges = exchange(
                ends, (groups, 2, 2, margin, width), counts, False, 2 + level_index
            )
            window = jnp.concatenate([edges[:, :, 0], image, edges[:, :, 1]], 2)
    return jnp.stack([real[0], imag[0]], 1)


def solution(mesh):
    in_specs = (
        P(("sub", "beam", "comp"), None, None),
        P(),
        P(None, ("sub", "beam", "comp")),
        P(None, ("beam", "comp")),
        P(None, ("beam", "comp"), None),
        P(None, ("beam", "comp")),
    )
    out_specs = P(("beam", "comp"), None, "sub")
    return jax.shard_map(body, mesh=mesh, in_specs=in_specs, out_specs=out_specs, check_vma=False)
```

time: 153 us -> 123 us (0.80)
  Pallas kernels: 59.3 us -> 85.4 us
  waiting for transfers between devices: 20.3 us -> 0 us
  starting transfers between devices: 15.6 us -> 0 us
  local copies, waits for them, and re-layouts: 21.7 us -> 7.12 us
  other arithmetic: 16.1 us -> 9.9 us
    pallas_call x0 -> x2, Pallas kernels: none -> 26.3 us  [exchange(): pl.pallas_call(functools.partial(exchange_kernel, counts, spread), out_sh...]
    ppermute x6 -> x0, waiting for transfers between devices: 20.3 us -> none  [the longest x2 7.65 us: with_halo(): lax.ppermute(lax.slice_in_dim(block, block.shape[dim] - width, None, axis...]
    ppermute x6 -> x0, starting transfers between devices: 15.6 us -> none  [the longest x2 9.57 us: with_halo(): lax.ppermute(lax.slice_in_dim(block, 0, width, axis=dim), axis, backward)]
    reshape x4 -> x2, local copies, waits for them, and re-layouts: 10.2 us -> 0.16 us  [compress(): first = real_form(RADIX).reshape(2, RADIX, 2, RADIX)]
    convert_element_type x1 -> x0, local copies, waits for them, and re-layouts: 6.5 us -> none  [body(): partial = beam_term(weights, raw_pulses).astype(jnp.bfloat16)]
    another operation x5 -> x7, other arithmetic: 5.32 us -> 1.6 us
    sub x0 -> x2, other arithmetic: none -> 2.03 us  [the longest x1 1.89 us: phases(): cosine = cos_one * cos_two - sin_one * sin_two]
    concatenate x2 -> x0, other arithmetic: 1.95 us -> none  [with_halo(): block = jnp.concatenate([low, block, high], axis=dim)]
  transfers between devices with their start and end apart: 6 -> 0, of which waited for: 6 -> 0; matrix products, arithmetic and copies ran while one was open for 1% -> 0% of each run, Pallas kernels for 0% -> 0%
where the time goes in v3:
time: 123 us; the launch traced here: 122 us
  Pallas kernels  85.4 us (69%)
  matrix products  19.4 us (16%)
  other arithmetic  9.9 us (8%)
  local copies, waits for them, and re-layouts  7.12 us (6%)
    pallas_call x1, Pallas kernels, reduce_beams(): pl.pallas_call(functools.partial(reduce_kernel, beam_count, comp_count),...  59.2 us
    pallas_call x2, Pallas kernels, exchange(): pl.pallas_call(functools.partial(exchange_kernel, counts, spread), out_sh...  26.3 us
    dot_general x1, matrix products, beam_term(): jnp.einsum('kspq,pqr->skr', weights, pulses, preferred_element_type=jnp.f...  15 us

profile of v3, /device:TPU:8, one launch (start us, length us, event | category | flops | bytes accessed | tf_op | source)
XLA Modules:
  0.0 122.2 jit_solution(9095632858794174212)
XLA Ops:
  0.0 0.9 fusion.34
  0.9 0.9 negate_bitcast_fusion
  1.8 15.0 %fusion = bf16[64,2,16384]{2,0,1:T(8,128)(2,1)} fusion(bf16[128,2,16384]{2,1,0:T(2,128)(2,1)} %param.6, bf16[64,1,128,2]{2,0,3,1:T(8,128)(2,1)S(1)} %get-tuple-element.38, bf16[64,1,128,2]{2,0,3,1:T(8,128)(2,1)S(1)} %get-tuple-element.37), kind=kOutput, calls=%fused_computation.1 | convolution fusion | flops 1075871744 | bytes 12648448 | tf_op jit(solution)/shard_map/kspq,pqr->skr/dot_general | solution.py:70
  16.8 59.2 %shard_map.64 = bf16[2,8,16384]{2,1,0:T(8,128)(2,1)} custom-call(bf16[2,4,2,8,16384]{4,3,2,1,0:T(8,128)(2,1)} %bitcast.176), custom_call_target="tpu_custom_call" | custom-call | tf_op jit(solution)/shard_map/pallas_call | solution.py:145
  76.0 0.3 negate_convert_fusion
  76.3 0.3 fusion.29
  76.6 0.1 copy.60
  76.8 1.5 %convolution_bitcast_fusion.7 = f32[2,8,128,128]{3,2,1,0:T(8,128)S(1)} fusion(bf16[2,128,2,128,1]{1,3,0,4,2:T(8,128)(2,1)S(1)} %copy.60, bf16[2,8,128,128]{3,1,2,0:T(8,128)(2,1)} %bitcast.177), kind=kOutput, calls=%fused_computation.12 | convolution fusion | flops 134217728 | bytes 1703936 | tf_op jit(solution)/shard_map/rpan,rask->spkn/dot_general | solution.py:43
  78.3 0.3 sine_negate_fusion
  78.5 0.1 multiply_subtract_fusion.1
  78.7 0.3 convolution_bitcast_fusion.5
  79.0 0.3 fusion.4
  79.5 0.2 squeeze.20
  79.7 0.2 squeeze.21
  79.9 0.4 copy-done.2
  80.4 0.1 fusion.45
  80.5 0.3 multiply_convert_fusion.1
  80.8 0.4 pad_maximum_fusion.2.image_ref
  81.2 16.4 %shard_map.65 = bf16[4,2,4,4,4096]{4,3,2,1,0:T(4,128)(2,1)S(1)} custom-call(bf16[2,2,4,16384]{3,2,1,0:T(4,128)(2,1)S(1)} %pad_maximum_fusion.2.image_ref), custom_call_target="tpu_custom_call" | custom-call | tf_op jit(solution)/shard_map/pallas_call | solution.py:293
  97.6 0.3 reshape_reshape.3
  98.0 0.1 copy.46
  98.1 0.1 select_reduce_fusion.3
  98.3 0.5 convolution_bitcast_fusion.4
  98.8 1.1 slice_add_fusion.3
  100.0 0.1 select_reduce_fusion.2
  100.2 0.5 convolution_bitcast_fusion.3
  100.8 1.1 slice_add_fusion.2
  101.9 0.2 multiply_cosine_fusion.1
  102.1 0.2 multiply_cosine_fusion
  102.4 1.9 %multiply_subtract_fusion = (f32[2,48,32,128]{3,2,1,0:T(8,128)}, f32[2,48,32,128]{3,2,1,0:T(8,128)S(1)}) fusion(f32[2,48,128]{2,1,0:T(8,128)S(1)} %get-tuple-element.46, f32[2,48,32]{2,1,0:T(8,128)S(1)} %get-tuple-element.44, f32[2,48,128]{2,1,0:T(8,128)S(1)} %get-tuple-element.45, f32[2,48,32]{2,1,0:T(8,128)S(1)} %get-tuple-element.43), kind=kLoop, calls=%fused_computation.9 | loop fusion | flops 2359296 | bytes 3268608 | tf_op jit(solution)/shard_map/sub | solution.py:311
  104.3 0.3 add.246
  104.6 1.6 %sub.52 = f32[2,48,4096]{2,1,0:T(8,128)S(1)} reshape(f32[2,48,32,128]{3,2,1,0:T(8,128)} %get-tuple-element.31) | data formatting | bytes 3145728 | tf_op jit(solution)/shard_map/sub | solution.py:311
  106.2 1.1 copy-done
  107.4 0.3 copy-done.1
  107.7 0.3 add_convert_fusion.1
  107.9 0.1 maximum_bitcast_fusion.1
  108.0 0.2 pad_maximum_fusion.3.image_ref
  108.2 9.9 %shard_map.66 = bf16[2,2,2,4,4096]{4,3,2,1,0:T(4,128)(2,1)S(1)} custom-call(bf16[2,2,2,4,4096]{4,3,2,1,0:T(4,128)(2,1)S(1)} %pad_maximum_fusion.3.image_ref), custom_call_target="tpu_custom_call" | custom-call | tf_op jit(solution)/shard_map/pallas_call | solution.py:293
  118.1 0.1 slice_bitcast_fusion.17
  118.2 0.3 maximum_bitcast_fusion
  118.5 0.1 slice_bitcast_fusion.18
  118.6 0.1 add_bitcast_fusion.2
  118.8 0.5 convolution_bitcast_fusion.1
  119.3 0.1 slice_add_fusion
  119.4 0.5 convolution_bitcast_fusion.2
  120.0 0.1 slice_add_fusion.1
  120.1 0.3 add_bitcast_fusion.1
  120.5 1.8 %copy.56 = f32[32,2,4096]{2,1,0:T(2,128)} copy(f32[32,2,4096]{2,0,1:T(8,128)S(1)} %pad_maximum_fusion.1) | data formatting | bytes 2097152 | tf_op jit(solution)/shard_map/stack | solution.py:372
  (30 shorter events, 0.7 us)
Async XLA Ops:
  79.5 0.9 copy-start.2
  81.2 16.7 %copy-start.5 = (s32[2,48]{1,0:T(2,128)S(1)}, s32[2,48]{1,0:T(2,128)}, u32[]{:S(2)}) copy-start(s32[2,48]{1,0:T(2,128)} %param.9) | copy-start | bytes 1156
  81.2 16.8 %copy-start.3 = (f32[2,48,8]{1,2,0:T(8,128)S(1)}, f32[2,48,8]{1,2,0:T(8,128)}, u32[]{:S(2)}) copy-start(f32[2,48,8]{1,2,0:T(8,128)} %param.10) | copy-start | bytes 9220
  100.8 1.1 copy-start.4
  106.1 1.2 %copy-start = (f32[2,2,16,4096]{3,2,1,0:T(8,128)S(1)}, f32[2,2,16,4096]{3,2,1,0:T(8,128)}, u32[]{:S(2)}) copy-start(f32[2,2,16,4096]{3,2,1,0:T(8,128)} %slice_add_fusion.3) | copy-start | bytes 3145732
  106.1 1.5 %copy-start.1 = (f32[2,2,16,4096]{3,2,1,0:T(8,128)S(1)}, f32[2,2,16,4096]{3,2,1,0:T(8,128)}, u32[]{:S(2)}) copy-start(f32[2,2,16,4096]{3,2,1,0:T(8,128)} %slice_add_fusion.2) | copy-start | bytes 3145732

commit v4 on v3

--- a/solution.py
+++ b/solution.py
@@ -12,6 +12,7 @@
 RADIX = 128
 BAND = 8
 CHUNKS = 8
+COMP_FIRST = 5
 MESH = pl.DeviceIdType.MESH
 
 
@@ -61,105 +62,143 @@
 def steering(phase_angle, factor):
     real_part = (jnp.cos(phase_angle) * factor).astype(jnp.bfloat16)
     imag_part = (jnp.sin(phase_angle) * factor).astype(jnp.bfloat16)
-    return jnp.stack(
-        [jnp.stack([real_part, -imag_part], -1), jnp.stack([imag_part, real_part], -1)], 1
-    )
-
-
-def beam_term(weights, pulses):
-    return jnp.einsum("kspq,pqr->skr", weights, pulses, preferred_element_type=jnp.float32)
+    upper_rows = jnp.stack([real_part, -imag_part], -1).reshape(phase_angle.shape[0], -1)
+    lower_rows = jnp.stack([imag_part, real_part], -1).reshape(phase_angle.shape[0], -1)
+    return jnp.concatenate([upper_rows, lower_rows], 0)
 
 
 def reduce_kernel(
-    beam_count, comp_count, part_ref, out_ref, recv_one, send_two, recv_two,
-    one_send, one_recv, two_send, two_recv,
+    beam_count, comp_count, comp_chunks, weight_ref, raw_ref, out_ref, raw, part, recv_one,
+    send_two, recv_two, load_sem, one_send, one_recv, two_send, two_recv,
 ):
-    z = lax.axis_index("beam")
-    y = lax.axis_index("comp")
-    width = part_ref.shape[-1] // CHUNKS
+    sizes = {"beam": beam_count, "comp": comp_count}
+    mine = {"beam": lax.axis_index("beam"), "comp": lax.axis_index("comp")}
+    rows = out_ref.shape[1]
+    width = raw_ref.shape[-1] // CHUNKS
+    loads = []
+    for j in range(CHUNKS):
+        cols = pl.ds(j * width, width)
+        loads.append(
+            pltpu.make_async_copy(raw_ref.at[:, :, cols], raw.at[:, :, cols], load_sem.at[j])
+        )
+        loads[j].start()
+
+    def peer_of(axis, d):
+        return lax.rem(mine[axis] + d, sizes[axis])
+
+    def route(j):
+        beams_before = j * (CHUNKS - comp_chunks) // CHUNKS
+        beams_after = (j + 1) * (CHUNKS - comp_chunks) // CHUNKS
+        return ("beam", "comp") if beams_after > beams_before else ("comp", "beam")
+
+    def owned(ref, axis, index, cols):
+        if axis == "comp":
+            return ref[:, :, index, :, cols]
+        return ref[:, index, :, :, cols]
+
     barrier = pltpu.get_barrier_semaphore()
-    for d in range(1, comp_count):
-        pl.semaphore_signal(
-            barrier, inc=1, device_id={"comp": lax.rem(y + d, comp_count)}, device_id_type=MESH
-        )
-    for d in range(1, beam_count):
-        pl.semaphore_signal(
-            barrier, inc=1, device_id={"beam": lax.rem(z + d, beam_count)}, device_id_type=MESH
-        )
+    for axis in sizes:
+        for d in range(1, sizes[axis]):
+            pl.semaphore_signal(
+                barrier, inc=1, device_id={axis: peer_of(axis, d)}, device_id_type=MESH
+            )
     pl.semaphore_wait(barrier, comp_count + beam_count - 2)
     first = []
     for j in range(CHUNKS):
         cols = pl.ds(j * width, width)
-        for d in range(1, comp_count):
-            peer = lax.rem(y + d, comp_count)
+        loads[j].wait()
+        pulses = raw[:, :, cols].reshape(-1, width)
+        product = jnp.dot(weight_ref[...], pulses, preferred_element_type=jnp.float32)
+        part[:, :, :, :, cols] = product.astype(jnp.bfloat16).reshape(
+            2, beam_count, comp_count, rows, width
+        )
+        axis, other = route(j)
+        group = []
+        for d in range(1, sizes[axis]):
+            peer = peer_of(axis, d)
+            source = (
+                part.at[:, :, peer, :, cols] if axis == "comp" else part.at[:, peer, :, :, cols]
+            )
             copy = pltpu.make_async_remote_copy(
-                src_ref=part_ref.at[:, :, peer, :, cols],
-                dst_ref=recv_one.at[d - 1, :, :, :, cols],
+                src_ref=source,
+                dst_ref=recv_one.at[d - 1, :, pl.ds(0, sizes[other]), :, cols],
                 send_sem=one_send.at[d - 1, j],
                 recv_sem=one_recv.at[d - 1, j],
-                device_id={"comp": peer},
+                device_id={axis: peer},
                 device_id_type=MESH,
             )
             copy.start()
-            first.append(copy)
+            group.append(copy)
+        first.append(group)
     second = []
     for j in range(CHUNKS):
         cols = pl.ds(j * width, width)
-        for copy in first[j * (comp_count - 1) : (j + 1) * (comp_count - 1)]:
+        axis, other = route(j)
+        for copy in first[j]:
             copy.wait_recv()
-        total = part_ref[:, :, y, :, cols].astype(jnp.float32)
-        for d in range(1, comp_count):
-            total += recv_one[d - 1, :, :, :, cols].astype(jnp.float32)
-        send_two[:, :, :, cols] = total.astype(jnp.bfloat16)
-        for d in range(1, beam_count):
-            peer = lax.rem(z + d, beam_count)
+        total = owned(part, axis, mine[axis], cols).astype(jnp.float32)
+        for d in range(1, sizes[axis]):
+            total += recv_one[d - 1, :, : sizes[other], :, cols].astype(jnp.float32)
+        send_two[:, : sizes[other], :, cols] = total.astype(jnp.bfloat16)
+        group = []
+        for d in range(1, sizes[other]):
+            peer = peer_of(other, d)
             copy = pltpu.make_async_remote_copy(
                 src_ref=send_two.at[:, peer, :, cols],
                 dst_ref=recv_two.at[d - 1, :, :, cols],
                 send_sem=two_send.at[d - 1, j],
                 recv_sem=two_recv.at[d - 1, j],
-                device_id={"beam": peer},
+                device_id={other: peer},
                 device_id_type=MESH,
             )
             copy.start()
-            second.append(copy)
+            group.append(copy)
+        second.append(group)
     for j in range(CHUNKS):
         cols = pl.ds(j * width, width)
-        for copy in second[j * (beam_count - 1) : (j + 1) * (beam_count - 1)]:
+        axis, other = route(j)
+        for copy in second[j]:
             copy.wait_recv()
-        total = part_ref[:, z, y, :, cols].astype(jnp.float32)
-        for d in range(1, comp_count):
-            total += recv_one[d - 1, :, z, :, cols].astype(jnp.float32)
-        for d in range(1, beam_count):
+        total = part[:, mine["beam"], mine["comp"], :, cols].astype(jnp.float32)
+        for d in range(1, sizes[axis]):
+            total += recv_one[d - 1, :, mine[other], :, cols].astype(jnp.float32)
+        for d in range(1, sizes[other]):
             total += recv_two[d - 1, :, :, cols].astype(jnp.float32)
         out_ref[:, :, cols] = total.astype(jnp.bfloat16)
-    for copy in first + second:
-        copy.wait_send()
-
-
-def reduce_beams(partial, beam_count, comp_count):
+    for group in first + second:
+        for copy in group:
+            copy.wait_send()
+
+
+def reduce_beams(weights, raw_pulses, beam_count, comp_count):
     blocks = beam_count * comp_count
-    rows = partial.shape[1] // blocks
-    length = partial.shape[2]
-    part = partial.reshape(2, beam_count, comp_count, rows, length)
+    rows = weights.shape[0] // (2 * blocks)
+    length = raw_pulses.shape[2]
+    most = max(beam_count, comp_count)
     return pl.pallas_call(
-        functools.partial(reduce_kernel, beam_count, comp_count),
+        functools.partial(reduce_kernel, beam_count, comp_count, COMP_FIRST),
         out_shape=jax.ShapeDtypeStruct((2, rows, length), jnp.bfloat16),
-        in_specs=[pl.BlockSpec(memory_space=pltpu.VMEM)],
+        in_specs=[
+            pl.BlockSpec(memory_space=pltpu.VMEM),
+            pl.BlockSpec(memory_space=pl.ANY),
+        ],
         out_specs=pl.BlockSpec(memory_space=pltpu.VMEM),
         scratch_shapes=[
-            pltpu.VMEM((comp_count - 1, 2, beam_count, rows, length), jnp.bfloat16),
-            pltpu.VMEM((2, beam_count, rows, length), jnp.bfloat16),
-            pltpu.VMEM((beam_count - 1, 2, rows, length), jnp.bfloat16),
-            pltpu.SemaphoreType.DMA((comp_count - 1, CHUNKS)),
-            pltpu.SemaphoreType.DMA((comp_count - 1, CHUNKS)),
-            pltpu.SemaphoreType.DMA((beam_count - 1, CHUNKS)),
-            pltpu.SemaphoreType.DMA((beam_count - 1, CHUNKS)),
+            pltpu.VMEM(raw_pulses.shape, jnp.bfloat16),
+            pltpu.VMEM((2, beam_count, comp_count, rows, length), jnp.bfloat16),
+            pltpu.VMEM((most - 1, 2, most, rows, length), jnp.bfloat16),
+            pltpu.VMEM((2, most, rows, length), jnp.bfloat16),
+            pltpu.VMEM((most - 1, 2, rows, length), jnp.bfloat16),
+            pltpu.SemaphoreType.DMA((CHUNKS,)),
+            pltpu.SemaphoreType.DMA((most - 1, CHUNKS)),
+            pltpu.SemaphoreType.DMA((most - 1, CHUNKS)),
+            pltpu.SemaphoreType.DMA((most - 1, CHUNKS)),
+            pltpu.SemaphoreType.DMA((most - 1, CHUNKS)),
         ],
         compiler_params=pltpu.CompilerParams(
-            collective_id=0, has_side_effects=True, vmem_limit_bytes=56 * 2**20
+            collective_id=0, has_side_effects=True, vmem_limit_bytes=60 * 2**20
         ),
-    )(part)
+    )(weights, raw_pulses)
 
 
 def band_matrix(offset, weight, span):
@@ -347,8 +386,7 @@
     start = lax.axis_index("sub") * width
     cosine, sine = phases(beam_delay, start, width)
     weights = steering(steer_angle, factor)
-    partial = beam_term(weights, raw_pulses).astype(jnp.bfloat16)
-    summed = reduce_beams(partial, beam_devices, comp_devices)
+    summed = reduce_beams(weights, raw_pulses, beam_devices, comp_devices)
     image = compress(summed, range_filter).astype(jnp.bfloat16)
     image = image.reshape(2, first_beams // margin, margin, NR)
     window = exchange(image, (sub_count, 2, 4, margin, width), counts, True, 1)

time: 123 us -> 123 us (level)
  matrix products: 19.4 us -> 4.19 us
  Pallas kernels: 85.4 us -> 96.9 us
  other arithmetic: 9.9 us -> 12 us
  local copies, waits for them, and re-layouts: 7.12 us -> 8.49 us
    dot_general x1 -> x0, matrix products: 15 us -> none  [beam_term(): jnp.einsum('kspq,pqr->skr', weights, pulses, preferred_element_type=jnp.f...]
    pallas_call x1, Pallas kernels: 59.2 us -> 69.5 us  [reduce_beams(): pl.pallas_call(functools.partial(reduce_kernel, beam_count, comp_count, C...]
    add x5, other arithmetic: 0.16 us -> 1.67 us  [band_matrix(): offset[:, None] + BAND // 2 + jnp.arange(BAND, dtype=jnp.int32)[None, :]]
    broadcast_in_dim x4, local copies, waits for them, and re-layouts: 0.22 us -> 1.63 us  [band_matrix(): jnp.where(matches, weight[:, :, None], jnp.zeros_like(weight)[:, :, None])]
    sub x1, local copies, waits for them, and re-layouts: 1.56 us -> 0.28 us  [phases(): cosine = cos_one * cos_two - sin_one * sin_two]
    add x1, local copies, waits for them, and re-layouts: 0.28 us -> 1.56 us  [phases(): sine = sin_one * cos_two + cos_one * sin_two]
where the time goes in v4:
time: 123 us; the launch traced here: 122 us
  Pallas kernels  96.9 us (79%)
  other arithmetic  12 us (10%)
  local copies, waits for them, and re-layouts  8.49 us (7%)
  matrix products  4.19 us (3%)
    pallas_call x1, Pallas kernels, reduce_beams(): pl.pallas_call(functools.partial(reduce_kernel, beam_count, comp_count, C...  69.5 us
    pallas_call x2, Pallas kernels, exchange(): pl.pallas_call(functools.partial(exchange_kernel, counts, spread), out_sh...  27.4 us

profile of v4, /device:TPU:8, one launch (start us, length us, event | category | flops | bytes accessed | tf_op | source)
XLA Modules:
  0.0 122.0 jit_solution(12128049978657966652)
XLA Ops:
  0.0 0.8 add_bitcast_fusion.2
  0.9 0.8 add_bitcast_fusion.5
  1.6 0.8 slice_bitcast_fusion.18
  2.5 0.7 slice_bitcast_fusion.21
  3.4 0.1 select_reduce_fusion.2
  3.6 0.1 select_reduce_fusion.3
  3.8 0.9 negate_bitcast_fusion
  4.7 0.3 fusion.23
  4.9 0.9 fusion.28
  5.8 0.1 copy.42
  6.1 0.1 copy.43
  6.3 0.6 pad_maximum_fusion.5.weight_ref
  6.9 0.3 negate_convert_fusion
  7.3 0.1 copy.66
  7.4 0.2 multiply_cosine_fusion
  7.7 0.2 multiply_cosine_fusion.1
  8.1 0.3 sine_negate_fusion
  8.3 69.5 %shard_map.64 = bf16[2,8,16384]{2,1,0:T(8,128)(2,1)} custom-call(bf16[128,256]{1,0:T(8,128)(2,1)} %pad_maximum_fusion.5.weight_ref, bf16[128,2,16384]{2,1,0:T(2,128)(2,1)} %raw_ref.1), custom_call_target="tpu_custom_call" | custom-call | tf_op jit(solution)/shard_map/pallas_call | solution.py:178
  77.9 1.3 %convolution_bitcast_fusion.6 = f32[2,8,128,128]{3,2,1,0:T(8,128)S(1)} fusion(bf16[2,128,2,128,1]{1,3,0,4,2:T(8,128)(2,1)S(1)} %copy.66, bf16[2,8,128,128]{3,1,2,0:T(8,128)(2,1)} %bitcast.163), kind=kOutput, calls=%fused_computation.8 | convolution fusion | flops 134217728 | bytes 1703936 | tf_op jit(solution)/shard_map/rpan,rask->spkn/dot_general | solution.py:44
  79.2 0.1 multiply_subtract_fusion.1
  79.3 0.3 convolution_bitcast_fusion.4
  79.7 0.3 fusion.1
  80.1 0.2 squeeze.20
  80.3 0.2 squeeze.21
  80.6 0.3 multiply_convert_fusion.1
  80.9 0.4 pad_maximum_fusion.2.image_ref
  81.3 17.4 %shard_map.65 = bf16[4,2,4,4,4096]{4,3,2,1,0:T(4,128)(2,1)S(1)} custom-call(bf16[2,2,4,16384]{3,2,1,0:T(4,128)(2,1)S(1)} %pad_maximum_fusion.2.image_ref), custom_call_target="tpu_custom_call" | custom-call | tf_op jit(solution)/shard_map/pallas_call | solution.py:332
  98.6 0.3 reshape_reshape.3
  98.9 0.5 convolution_bitcast_fusion.3
  99.5 1.1 slice_add_fusion.3
  100.6 0.5 convolution_bitcast_fusion.2
  101.1 1.1 slice_add_fusion.2
  102.2 1.9 %multiply_subtract_fusion = (f32[2,48,32,128]{3,2,1,0:T(8,128)S(1)}, f32[2,48,32,128]{3,2,1,0:T(8,128)}) fusion(f32[2,48,128]{2,1,0:T(8,128)S(1)} %get-tuple-element.46, f32[2,48,32]{2,1,0:T(8,128)S(1)} %get-tuple-element.44, f32[2,48,128]{2,1,0:T(8,128)S(1)} %get-tuple-element.45, f32[2,48,32]{2,1,0:T(8,128)S(1)} %get-tuple-element.43), kind=kLoop, calls=%fused_computation.5 | loop fusion | flops 2359296 | bytes 3268608 | tf_op jit(solution)/shard_map/sub | solution.py:350
  104.1 0.3 sub.52
  104.4 1.6 %add.246 = f32[2,48,4096]{2,1,0:T(8,128)S(1)} reshape(f32[2,48,32,128]{3,2,1,0:T(8,128)} %get-tuple-element.32) | data formatting | bytes 3145728 | tf_op jit(solution)/shard_map/add | solution.py:351
  106.0 1.1 copy-done
  107.2 0.3 copy-done.1
  107.5 0.3 add_convert_fusion.1
  107.7 0.1 maximum_bitcast_fusion.1
  107.9 0.2 pad_maximum_fusion.3.image_ref
  108.0 10.1 %shard_map.66 = bf16[2,2,2,4,4096]{4,3,2,1,0:T(4,128)(2,1)S(1)} custom-call(bf16[2,2,2,4,4096]{4,3,2,1,0:T(4,128)(2,1)S(1)} %pad_maximum_fusion.3.image_ref), custom_call_target="tpu_custom_call" | custom-call | tf_op jit(solution)/shard_map/pallas_call | solution.py:332
  118.2 0.3 maximum_bitcast_fusion
  118.5 0.5 convolution_bitcast_fusion
  119.1 0.1 slice_add_fusion
  119.2 0.5 convolution_bitcast_fusion.1
  119.7 0.1 slice_add_fusion.1
  119.9 0.3 add_bitcast_fusion.1
  120.2 1.8 %copy.63 = f32[32,2,4096]{2,1,0:T(2,128)} copy(f32[32,2,4096]{2,0,1:T(8,128)S(1)} %pad_maximum_fusion.1) | data formatting | bytes 2097152 | tf_op jit(solution)/shard_map/stack | solution.py:410
  (30 shorter events, 1.1 us)
Async XLA Ops:
  0.0 7.4 %copy-start.3 = (f32[2,48]{1,0:T(2,128)S(1)}, f32[2,48]{1,0:T(2,128)}, u32[]{:S(2)}) copy-start(f32[2,48]{1,0:T(2,128)} %param.11) | copy-start | bytes 1156
  0.0 7.9 %copy-start.2 = (f32[2,16384]{1,0:T(2,128)S(1)}, f32[2,16384]{1,0:T(2,128)}, u32[]{:S(2)}) copy-start(f32[2,16384]{1,0:T(2,128)} %param.7) | copy-start | bytes 393220
  105.9 1.2 %copy-start = (f32[2,2,16,4096]{3,2,1,0:T(8,128)S(1)}, f32[2,2,16,4096]{3,2,1,0:T(8,128)}, u32[]{:S(2)}) copy-start(f32[2,2,16,4096]{3,2,1,0:T(8,128)} %slice_add_fusion.3) | copy-start | bytes 3145732
  105.9 1.5 %copy-start.1 = (f32[2,2,16,4096]{3,2,1,0:T(8,128)S(1)}, f32[2,2,16,4096]{3,2,1,0:T(8,128)}, u32[]{:S(2)}) copy-start(f32[2,2,16,4096]{3,2,1,0:T(8,128)} %slice_add_fusion.2) | copy-start | bytes 3145732

commit v5 on v4

--- a/solution.py
+++ b/solution.py
@@ -11,8 +11,8 @@
 NR = 16384
 RADIX = 128
 BAND = 8
-CHUNKS = 8
-COMP_FIRST = 5
+CHUNKS = 16
+COMP_FIRST = CHUNKS
 MESH = pl.DeviceIdType.MESH
 
 

time: 123 us -> 110 us (0.89)
  Pallas kernels: 96.9 us -> 84.4 us
    pallas_call x1, Pallas kernels: 69.5 us -> 58 us  [reduce_beams(): pl.pallas_call(functools.partial(reduce_kernel, beam_count, comp_count, C...]
where the time goes in v5:
time: 110 us; the launch traced here: 109 us
  Pallas kernels  84.4 us (77%)
  other arithmetic  12 us (11%)
  local copies, waits for them, and re-layouts  8.49 us (8%)
  matrix products  4.19 us (4%)
    pallas_call x1, Pallas kernels, reduce_beams(): pl.pallas_call(functools.partial(reduce_kernel, beam_count, comp_count, C...  58 us
    pallas_call x2, Pallas kernels, exchange(): pl.pallas_call(functools.partial(exchange_kernel, counts, spread), out_sh...  26.4 us
    add x4, other arithmetic, merge(): blended = blended[:, :, :count] + blended[:, :, count:]  2.4 us

profile of v5, /device:TPU:8, one launch (start us, length us, event | category | flops | bytes accessed | tf_op | source)
XLA Modules:
  0.0 109.5 jit_solution(1095375565267645962)
XLA Ops:
  0.0 0.8 add_bitcast_fusion.2
  0.9 0.8 add_bitcast_fusion.5
  1.6 0.8 slice_bitcast_fusion.18
  2.5 0.7 slice_bitcast_fusion.21
  3.4 0.1 select_reduce_fusion.2
  3.6 0.1 select_reduce_fusion.3
  3.8 0.9 negate_bitcast_fusion
  4.7 0.3 fusion.23
  4.9 0.9 fusion.28
  5.8 0.1 copy.42
  6.1 0.1 copy.43
  6.3 0.6 pad_maximum_fusion.5.weight_ref
  6.9 0.3 negate_convert_fusion
  7.3 0.1 copy.66
  7.4 0.2 multiply_cosine_fusion
  7.7 0.2 multiply_cosine_fusion.1
  8.1 0.3 sine_negate_fusion
  8.3 58.0 %shard_map.64 = bf16[2,8,16384]{2,1,0:T(8,128)(2,1)} custom-call(bf16[128,256]{1,0:T(8,128)(2,1)} %pad_maximum_fusion.5.weight_ref, bf16[128,2,16384]{2,1,0:T(2,128)(2,1)} %raw_ref.1), custom_call_target="tpu_custom_call" | custom-call | tf_op jit(solution)/shard_map/pallas_call | solution.py:178
  66.4 1.3 %convolution_bitcast_fusion.6 = f32[2,8,128,128]{3,2,1,0:T(8,128)S(1)} fusion(bf16[2,128,2,128,1]{1,3,0,4,2:T(8,128)(2,1)S(1)} %copy.66, bf16[2,8,128,128]{3,1,2,0:T(8,128)(2,1)} %bitcast.163), kind=kOutput, calls=%fused_computation.8 | convolution fusion | flops 134217728 | bytes 1703936 | tf_op jit(solution)/shard_map/rpan,rask->spkn/dot_general | solution.py:44
  67.7 0.1 multiply_subtract_fusion.1
  67.9 0.3 convolution_bitcast_fusion.4
  68.2 0.3 fusion.1
  68.6 0.2 squeeze.20
  68.9 0.2 squeeze.21
  69.1 0.3 multiply_convert_fusion.1
  69.4 0.4 pad_maximum_fusion.2.image_ref
  69.8 16.6 %shard_map.65 = bf16[4,2,4,4,4096]{4,3,2,1,0:T(4,128)(2,1)S(1)} custom-call(bf16[2,2,4,16384]{3,2,1,0:T(4,128)(2,1)S(1)} %pad_maximum_fusion.2.image_ref), custom_call_target="tpu_custom_call" | custom-call | tf_op jit(solution)/shard_map/pallas_call | solution.py:332
  86.4 0.3 reshape_reshape.3
  86.7 0.5 convolution_bitcast_fusion.3
  87.2 1.1 %slice_add_fusion.3 = f32[2,2,16,4096]{3,2,1,0:T(8,128)} fusion(f32[2,2,32,4096]{3,2,1,0:T(8,128)S(1)} %convolution_bitcast_fusion.3), kind=kLoop, calls=%fused_computation.14 | loop fusion | flops 262144 | bytes 3145728 | tf_op jit(solution)/shard_map/add | solution.py:369
  88.3 0.5 convolution_bitcast_fusion.2
  88.9 1.1 slice_add_fusion.2
  90.0 1.9 %multiply_subtract_fusion = (f32[2,48,32,128]{3,2,1,0:T(8,128)S(1)}, f32[2,48,32,128]{3,2,1,0:T(8,128)}) fusion(f32[2,48,128]{2,1,0:T(8,128)S(1)} %get-tuple-element.46, f32[2,48,32]{2,1,0:T(8,128)S(1)} %get-tuple-element.44, f32[2,48,128]{2,1,0:T(8,128)S(1)} %get-tuple-element.45, f32[2,48,32]{2,1,0:T(8,128)S(1)} %get-tuple-element.43), kind=kLoop, calls=%fused_computation.5 | loop fusion | flops 2359296 | bytes 3268608 | tf_op jit(solution)/shard_map/sub | solution.py:350
  91.8 0.3 sub.52
  92.1 1.6 %add.246 = f32[2,48,4096]{2,1,0:T(8,128)S(1)} reshape(f32[2,48,32,128]{3,2,1,0:T(8,128)} %get-tuple-element.32) | data formatting | bytes 3145728 | tf_op jit(solution)/shard_map/add | solution.py:351
  93.8 1.1 %copy-done = f32[2,2,16,4096]{3,2,1,0:T(8,128)S(1)} copy-done((f32[2,2,16,4096]{3,2,1,0:T(8,128)S(1)}, f32[2,2,16,4096]{3,2,1,0:T(8,128)}, u32[]{:S(2)}) %copy-start) | copy-done | bytes 1048600
  94.9 0.3 copy-done.1
  95.2 0.3 add_convert_fusion.1
  95.5 0.1 maximum_bitcast_fusion.1
  95.6 0.2 pad_maximum_fusion.3.image_ref
  95.8 9.8 %shard_map.66 = bf16[2,2,2,4,4096]{4,3,2,1,0:T(4,128)(2,1)S(1)} custom-call(bf16[2,2,2,4,4096]{4,3,2,1,0:T(4,128)(2,1)S(1)} %pad_maximum_fusion.3.image_ref), custom_call_target="tpu_custom_call" | custom-call | tf_op jit(solution)/shard_map/pallas_call | solution.py:332
  105.7 0.3 maximum_bitcast_fusion
  106.0 0.5 convolution_bitcast_fusion
  106.6 0.1 slice_add_fusion
  106.7 0.5 convolution_bitcast_fusion.1
  107.2 0.1 slice_add_fusion.1
  107.3 0.3 add_bitcast_fusion.1
  107.7 1.8 %copy.63 = f32[32,2,4096]{2,1,0:T(2,128)} copy(f32[32,2,4096]{2,0,1:T(8,128)S(1)} %pad_maximum_fusion.1) | data formatting | bytes 2097152 | tf_op jit(solution)/shard_map/stack | solution.py:410
  (30 shorter events, 1.1 us)
Async XLA Ops:
  0.0 7.4 %copy-start.3 = (f32[2,48]{1,0:T(2,128)S(1)}, f32[2,48]{1,0:T(2,128)}, u32[]{:S(2)}) copy-start(f32[2,48]{1,0:T(2,128)} %param.11) | copy-start | bytes 1156
  0.0 7.9 %copy-start.2 = (f32[2,16384]{1,0:T(2,128)S(1)}, f32[2,16384]{1,0:T(2,128)}, u32[]{:S(2)}) copy-start(f32[2,16384]{1,0:T(2,128)} %param.7) | copy-start | bytes 393220
  93.7 1.2 %copy-start = (f32[2,2,16,4096]{3,2,1,0:T(8,128)S(1)}, f32[2,2,16,4096]{3,2,1,0:T(8,128)}, u32[]{:S(2)}) copy-start(f32[2,2,16,4096]{3,2,1,0:T(8,128)} %slice_add_fusion.3) | copy-start | bytes 3145732
  93.7 1.5 %copy-start.1 = (f32[2,2,16,4096]{3,2,1,0:T(8,128)S(1)}, f32[2,2,16,4096]{3,2,1,0:T(8,128)}, u32[]{:S(2)}) copy-start(f32[2,2,16,4096]{3,2,1,0:T(8,128)} %slice_add_fusion.2) | copy-start | bytes 3145732

commit v6 on v5

--- a/solution.py
+++ b/solution.py
@@ -13,6 +13,7 @@
 BAND = 8
 CHUNKS = 16
 COMP_FIRST = CHUNKS
+LAG = 3
 MESH = pl.DeviceIdType.MESH
 
 
@@ -104,7 +105,9 @@
             )
     pl.semaphore_wait(barrier, comp_count + beam_count - 2)
     first = []
-    for j in range(CHUNKS):
+    second = []
+
+    def start_first(j):
         cols = pl.ds(j * width, width)
         loads[j].wait()
         pulses = raw[:, :, cols].reshape(-1, width)
@@ -130,8 +133,8 @@
             copy.start()
             group.append(copy)
         first.append(group)
-    second = []
-    for j in range(CHUNKS):
+
+    def start_second(j):
         cols = pl.ds(j * width, width)
         axis, other = route(j)
         for copy in first[j]:
@@ -154,6 +157,12 @@
             copy.start()
             group.append(copy)
         second.append(group)
+
+    for j in range(CHUNKS + LAG):
+        if j < CHUNKS:
+            start_first(j)
+        if j >= LAG:
+            start_second(j - LAG)
     for j in range(CHUNKS):
         cols = pl.ds(j * width, width)
         axis, other = route(j)

time: 110 us -> 110 us (level)
  no operation moved by 1% of the time
where the time goes in v6:
time: 110 us; the launch traced here: 109 us
  Pallas kernels  84.3 us (77%)
  other arithmetic  12 us (11%)
  local copies, waits for them, and re-layouts  8.49 us (8%)
  matrix products  4.19 us (4%)
    pallas_call x1, Pallas kernels, reduce_beams(): pl.pallas_call(functools.partial(reduce_kernel, beam_count, comp_count, C...  58 us
    pallas_call x2, Pallas kernels, exchange(): pl.pallas_call(functools.partial(exchange_kernel, counts, spread), out_sh...  26.2 us
    add x4, other arithmetic, merge(): blended = blended[:, :, :count] + blended[:, :, count:]  2.4 us

profile of v6, /device:TPU:8, one launch (start us, length us, event | category | flops | bytes accessed | tf_op | source)
XLA Modules:
  0.0 109.3 jit_solution(7890050611976434907)
XLA Ops:
  0.0 0.8 add_bitcast_fusion.2
  0.9 0.8 add_bitcast_fusion.5
  1.6 0.8 slice_bitcast_fusion.18
  2.5 0.7 slice_bitcast_fusion.21
  3.4 0.1 select_reduce_fusion.2
  3.6 0.1 select_reduce_fusion.3
  3.8 0.9 negate_bitcast_fusion
  4.7 0.3 fusion.23
  4.9 0.9 fusion.28
  5.8 0.1 copy.42
  6.1 0.1 copy.43
  6.3 0.6 pad_maximum_fusion.5.weight_ref
  6.9 0.3 negate_convert_fusion
  7.3 0.1 copy.66
  7.4 0.2 multiply_cosine_fusion
  7.7 0.2 multiply_cosine_fusion.1
  8.1 0.3 sine_negate_fusion
  8.3 58.0 %shard_map.64 = bf16[2,8,16384]{2,1,0:T(8,128)(2,1)} custom-call(bf16[128,256]{1,0:T(8,128)(2,1)} %pad_maximum_fusion.5.weight_ref, bf16[128,2,16384]{2,1,0:T(2,128)(2,1)} %raw_ref.1), custom_call_target="tpu_custom_call" | custom-call | tf_op jit(solution)/shard_map/pallas_call | solution.py:187
  66.4 1.3 %convolution_bitcast_fusion.6 = f32[2,8,128,128]{3,2,1,0:T(8,128)S(1)} fusion(bf16[2,128,2,128,1]{1,3,0,4,2:T(8,128)(2,1)S(1)} %copy.66, bf16[2,8,128,128]{3,1,2,0:T(8,128)(2,1)} %bitcast.163), kind=kOutput, calls=%fused_computation.8 | convolution fusion | flops 134217728 | bytes 1703936 | tf_op jit(solution)/shard_map/rpan,rask->spkn/dot_general | solution.py:45
  67.7 0.1 multiply_subtract_fusion.1
  67.9 0.3 convolution_bitcast_fusion.4
  68.2 0.3 fusion.1
  68.6 0.2 squeeze.20
  68.9 0.2 squeeze.21
  69.1 0.3 multiply_convert_fusion.1
  69.4 0.4 pad_maximum_fusion.2.image_ref
  69.8 16.3 %shard_map.65 = bf16[4,2,4,4,4096]{4,3,2,1,0:T(4,128)(2,1)S(1)} custom-call(bf16[2,2,4,16384]{3,2,1,0:T(4,128)(2,1)S(1)} %pad_maximum_fusion.2.image_ref), custom_call_target="tpu_custom_call" | custom-call | tf_op jit(solution)/shard_map/pallas_call | solution.py:341
  86.2 0.3 reshape_reshape.3
  86.5 0.5 convolution_bitcast_fusion.3
  87.0 1.1 %slice_add_fusion.3 = f32[2,2,16,4096]{3,2,1,0:T(8,128)} fusion(f32[2,2,32,4096]{3,2,1,0:T(8,128)S(1)} %convolution_bitcast_fusion.3), kind=kLoop, calls=%fused_computation.14 | loop fusion | flops 262144 | bytes 3145728 | tf_op jit(solution)/shard_map/add | solution.py:378
  88.1 0.5 convolution_bitcast_fusion.2
  88.7 1.1 slice_add_fusion.2
  89.7 1.9 %multiply_subtract_fusion = (f32[2,48,32,128]{3,2,1,0:T(8,128)S(1)}, f32[2,48,32,128]{3,2,1,0:T(8,128)}) fusion(f32[2,48,128]{2,1,0:T(8,128)S(1)} %get-tuple-element.46, f32[2,48,32]{2,1,0:T(8,128)S(1)} %get-tuple-element.44, f32[2,48,128]{2,1,0:T(8,128)S(1)} %get-tuple-element.45, f32[2,48,32]{2,1,0:T(8,128)S(1)} %get-tuple-element.43), kind=kLoop, calls=%fused_computation.5 | loop fusion | flops 2359296 | bytes 3268608 | tf_op jit(solution)/shard_map/sub | solution.py:359
  91.6 0.3 sub.52
  91.9 1.6 %add.246 = f32[2,48,4096]{2,1,0:T(8,128)S(1)} reshape(f32[2,48,32,128]{3,2,1,0:T(8,128)} %get-tuple-element.32) | data formatting | bytes 3145728 | tf_op jit(solution)/shard_map/add | solution.py:360
  93.6 1.1 %copy-done = f32[2,2,16,4096]{3,2,1,0:T(8,128)S(1)} copy-done((f32[2,2,16,4096]{3,2,1,0:T(8,128)S(1)}, f32[2,2,16,4096]{3,2,1,0:T(8,128)}, u32[]{:S(2)}) %copy-start) | copy-done | bytes 1048600
  94.7 0.3 copy-done.1
  95.0 0.3 add_convert_fusion.1
  95.3 0.1 maximum_bitcast_fusion.1
  95.4 0.2 pad_maximum_fusion.3.image_ref
  95.6 9.9 %shard_map.66 = bf16[2,2,2,4,4096]{4,3,2,1,0:T(4,128)(2,1)S(1)} custom-call(bf16[2,2,2,4,4096]{4,3,2,1,0:T(4,128)(2,1)S(1)} %pad_maximum_fusion.3.image_ref), custom_call_target="tpu_custom_call" | custom-call | tf_op jit(solution)/shard_map/pallas_call | solution.py:341
  105.6 0.3 maximum_bitcast_fusion
  105.9 0.5 convolution_bitcast_fusion
  106.4 0.1 slice_add_fusion
  106.5 0.5 convolution_bitcast_fusion.1
  107.1 0.1 slice_add_fusion.1
  107.2 0.3 add_bitcast_fusion.1
  107.6 1.8 %copy.63 = f32[32,2,4096]{2,1,0:T(2,128)} copy(f32[32,2,4096]{2,0,1:T(8,128)S(1)} %pad_maximum_fusion.1) | data formatting | bytes 2097152 | tf_op jit(solution)/shard_map/stack | solution.py:419
  (30 shorter events, 1.1 us)
Async XLA Ops:
  0.0 7.4 %copy-start.3 = (f32[2,48]{1,0:T(2,128)S(1)}, f32[2,48]{1,0:T(2,128)}, u32[]{:S(2)}) copy-start(f32[2,48]{1,0:T(2,128)} %param.11) | copy-start | bytes 1156
  0.0 7.9 %copy-start.2 = (f32[2,16384]{1,0:T(2,128)S(1)}, f32[2,16384]{1,0:T(2,128)}, u32[]{:S(2)}) copy-start(f32[2,16384]{1,0:T(2,128)} %param.7) | copy-start | bytes 393220
  93.5 1.2 %copy-start = (f32[2,2,16,4096]{3,2,1,0:T(8,128)S(1)}, f32[2,2,16,4096]{3,2,1,0:T(8,128)}, u32[]{:S(2)}) copy-start(f32[2,2,16,4096]{3,2,1,0:T(8,128)} %slice_add_fusion.3) | copy-start | bytes 3145732
  93.5 1.5 %copy-start.1 = (f32[2,2,16,4096]{3,2,1,0:T(8,128)S(1)}, f32[2,2,16,4096]{3,2,1,0:T(8,128)}, u32[]{:S(2)}) copy-start(f32[2,2,16,4096]{3,2,1,0:T(8,128)} %slice_add_fusion.2) | copy-start | bytes 3145732
